TPU v7x, 32 devices: a whole 2x2x4 slice. The times are simulated.
32 devices in a mesh: rep: 16 (over z, y, x), shard: 2 (over core).
Axes of the slice: x: 2, y: 2, z: 4, core: 2. Of those that a mesh axis runs over, the one named last changes fastest.
Arguments:
- tokens_in: bfloat16 [8192, 768], P(('rep', 'shard')), may hold values from -6 to 6
- cotangent: bfloat16 [8192, 768], P(('rep', 'shard')), may hold values from -6 to 6
- seq_lengths: int32 [32, 4], P(('rep', 'shard')), may hold values from 1 to 128, 256 in all within a row
- live_counts: int32 [32], P(('rep', 'shard')), may hold values from 64 to 256, as said below
- ln1_gain: bfloat16 [768], P('shard'), may hold values from 0.5 to 1.5
- ln1_shift: bfloat16 [768], P('shard'), may hold values from -3 to 3
- w_qkv: bfloat16 [768, 2304], P('shard'), may hold values from -0.21875 to 0.21875
- q_bias: bfloat16 [768], P('shard'), may hold values from -3 to 3
- v_bias: bfloat16 [768], P('shard'), may hold values from -3 to 3
- w_out: bfloat16 [768, 768], P('shard'), may hold values from -0.4375 to 0.4375
- out_bias: bfloat16 [768], P('shard'), may hold values from -3 to 3
- ln2_gain: bfloat16 [768], P('shard'), may hold values from 0.5 to 1.5
- ln2_shift: bfloat16 [768], P('shard'), may hold values from -3 to 3
- w_up: bfloat16 [768, 3072], P(None, 'shard'), may hold values from -0.21875 to 0.21875
- up_bias: bfloat16 [3072], P('shard'), may hold values from -3 to 3
- w_down: bfloat16 [3072, 768], P('shard'), may hold values from -0.109375 to 0.109375
- down_bias: bfloat16 [768], P('shard'), may hold values from -3 to 3
Outputs:
- block_out: bfloat16 [8192, 768], P(('rep', 'shard'))
- grad_tokens: bfloat16 [8192, 768], P(('rep', 'shard'))
- grad_ln1_gain: float32 [768], P('shard')
- grad_ln1_shift: float32 [768], P('shard')
- grad_w_qkv: float32 [768, 2304], P('shard')
- grad_q_bias: float32 [768], P('shard')
- grad_v_bias: float32 [768], P('shard')
- grad_w_out: float32 [768, 768], P('shard')
- grad_out_bias: float32 [768], P('shard')
- grad_ln2_gain: float32 [768], P('shard')
- grad_ln2_shift: float32 [768], P('shard')
- grad_w_up: float32 [768, 3072], P(None, 'shard')
- grad_up_bias: float32 [3072], P('shard')
- grad_w_down: float32 [3072, 768], P('shard')
- grad_down_bias: float32 [768], P('shard')
Inputs may be any that keep to these rules, and one draw needn't show every extreme that they name: `live_counts`: each device's live slots; some device has all 256 live in every draw. `seq_lengths`: each row sums to 256.
All inputs are finite; a program needn't handle non-finite values.
Results may differ from a plain program's by a relative error of at most 0.012.
Values may be sent and summed in bfloat16 or wider, within the bound.
No kernel may reach another device: no remote copies, remote signals or barrier semaphores. Data moves between devices by JAX's collectives and lax.ppermute only.
A program may use at most 192 MiB of HBM per device.

v0:
```python
import jax
import jax.numpy as jnp
from jax import lax
from jax.sharding import PartitionSpec as P

HEAD_DIM = 64


epsilon_norm = 1e-05
masked_score = -1e30


def matmul(left, right):
    return jnp.dot(left, right, preferred_element_type=jnp.float32)


def contract(form, left, right):
    return jnp.einsum(form, left, right, preferred_element_type=jnp.float32)


def norm_forward(values, gain, shift):
    center = values - jnp.mean(values, -1, keepdims=True)
    inverse = lax.rsqrt(jnp.mean(center * center, -1, keepdims=True) + epsilon_norm)
    normed = center * inverse
    return (normed * gain + shift, normed, inverse)


def norm_backward(upstream, normed, inverse, gain):
    scaled = upstream * gain
    inward = inverse * (
        scaled
        - jnp.mean(scaled, -1, keepdims=True)
        - normed * jnp.mean(scaled * normed, -1, keepdims=True)
    )
    return (inward, jnp.sum(upstream * normed, 0), jnp.sum(upstream, 0))


def live_mask(length_row, live_count, row_count):
    position = jnp.arange(row_count, dtype=jnp.int32)
    bounds = jnp.cumsum(length_row)
    segment = jnp.sum((position[:, None] >= bounds[None, :]).astype(jnp.int32), 1)
    live = position < live_count
    allowed = (segment[:, None] == segment[None, :]) & (position[None, :] <= position[:, None])
    allowed = allowed & (live[None, :] | (position[:, None] == position[None, :]))
    return (allowed, live)


def gelu_tanh(values):
    return jax.nn.gelu(values, approximate=True)


def score_block(query, keys, allowed):
    scores = contract("qhd,khd->hqk", query, keys) * query.shape[-1] ** (-0.5)
    return jnp.where(allowed[None], scores, masked_score)


def layer_pass(block_in, block_cot, length_row, live_count, forward_params, backward_params):
    (
        gain_one,
        shift_one,
        weight_qkv,
        bias_query,
        bias_value,
        weight_out,
        bias_out,
        gain_two,
        shift_two,
        weight_up,
        bias_up,
        weight_down,
        bias_down,
    ) = forward_params
    row_count = block_in.shape[0]
    width = block_in.shape[1]
    head_count = width // HEAD_DIM
    allowed, live = live_mask(length_row, live_count, row_count)
    live_col = live[:, None].astype(jnp.float32)
    tokens_f = block_in.astype(jnp.float32)
    normed_in, normed_one, inverse_one = norm_forward(
        tokens_f, gain_one.astype(jnp.float32), shift_one.astype(jnp.float32)
    )
    hidden_one = normed_in.astype(jnp.bfloat16)
    bias_full = jnp.concatenate(
        [
            bias_query.astype(jnp.float32),
            jnp.zeros((width,), jnp.float32),
            bias_value.astype(jnp.float32),
        ]
    )
    qkv = (matmul(hidden_one, weight_qkv) + bias_full).astype(jnp.bfloat16)
    query = qkv[:, :width].reshape(row_count, head_count, HEAD_DIM)
    keys = qkv[:, width : 2 * width].reshape(row_count, head_count, HEAD_DIM)
    value = qkv[:, 2 * width :].reshape(row_count, head_count, HEAD_DIM)
    scores = score_block(query, keys, allowed)
    highest = jnp.max(scores, -1, keepdims=True)
    logsum = highest + jnp.log(jnp.sum(jnp.exp(scores - highest), -1, keepdims=True))
    probs_b = jnp.exp(scores - logsum).astype(jnp.bfloat16)
    context = (
        contract("hqk,khd->qhd", probs_b, value).reshape(row_count, width).astype(jnp.bfloat16)
    )
    resid = tokens_f + matmul(context, weight_out) + bias_out.astype(jnp.float32)
    normed_mid, normed_two, inverse_two = norm_forward(
        resid, gain_two.astype(jnp.float32), shift_two.astype(jnp.float32)
    )
    hidden_two = normed_mid.astype(jnp.bfloat16)
    upper = matmul(hidden_two, weight_up) + bias_up.astype(jnp.float32)
    active, gelu_pull = jax.vjp(gelu_tanh, upper)
    active_b = active.astype(jnp.bfloat16)
    result = (
        (resid + matmul(active_b, weight_down) + bias_down.astype(jnp.float32)) * live_col
    ).astype(jnp.bfloat16)
    (
        gain_one,
        shift_one,
        weight_qkv,
        bias_query,
        bias_value,
        weight_out,
        bias_out,
        gain_two,
        shift_two,
        weight_up,
        bias_up,
        weight_down,
        bias_down,
    ) = backward_params
    grad_out = block_cot.astype(jnp.float32) * live_col
    grad_out_b = grad_out.astype(jnp.bfloat16)
    grad_wdown = matmul(active_b.T, grad_out_b)
    grad_bdown = jnp.sum(grad_out, 0)
    grad_upper = gelu_pull(matmul(grad_out_b, weight_down.T))[0]
    grad_upper_b = grad_upper.astype(jnp.bfloat16)
    grad_wup = matmul(hidden_two.T, grad_upper_b)
    grad_bup = jnp.sum(grad_upper, 0)
    grad_hidden_two = matmul(grad_upper_b, weight_up.T)
    grad_resid_norm, grad_gain_two, grad_shift_two = norm_backward(
        grad_hidden_two, normed_two, inverse_two, gain_two.astype(jnp.float32)
    )
    grad_resid = grad_out + grad_resid_norm
    grad_resid_b = grad_resid.astype(jnp.bfloat16)
    grad_wout = matmul(context.T, grad_resid_b)
    grad_bout = jnp.sum(grad_resid, 0)
    grad_context = (
        matmul(grad_resid_b, weight_out.T)
        .astype(jnp.bfloat16)
        .reshape(row_count, head_count, HEAD_DIM)
    )
    probs_again = jnp.exp(score_block(query, keys, allowed) - logsum)
    probs_again_b = probs_again.astype(jnp.bfloat16)
    grad_probs = contract("qhd,khd->hqk", grad_context, value)
    delta = jnp.sum(probs_again * grad_probs, -1, keepdims=True)
    grad_scores = (probs_again * (grad_probs - delta) * HEAD_DIM ** (-0.5)).astype(jnp.bfloat16)
    grad_query = contract("hqk,khd->qhd", grad_scores, keys).reshape(row_count, width)
    grad_keys = contract("hqk,qhd->khd", grad_scores, query).reshape(row_count, width)
    grad_value = contract("hqk,qhd->khd", probs_again_b, grad_context).reshape(row_count, width)
    grad_qkv = jnp.concatenate([grad_query, grad_keys, grad_value], 1).astype(jnp.bfloat16)
    grad_bquery = jnp.sum(grad_query, 0)
    grad_bvalue = jnp.sum(grad_value, 0)
    grad_wqkv = matmul(hidden_one.T, grad_qkv)
    grad_hidden_one = matmul(grad_qkv, weight_qkv.T)
    grad_in_norm, grad_gain_one, grad_shift_one = norm_backward(
        grad_hidden_one, normed_one, inverse_one, gain_one.astype(jnp.float32)
    )
    grad_in = (grad_resid + grad_in_norm).astype(jnp.bfloat16)
    gradients = (
        grad_gain_one,
        grad_shift_one,
        grad_wqkv,
        grad_bquery,
        grad_bvalue,
        grad_wout,
        grad_bout,
        grad_gain_two,
        grad_shift_two,
        grad_wup,
        grad_bup,
        grad_wdown,
        grad_bdown,
    )
    return (result, grad_in, gradients)


def local(
    tokens_in,
    cotangent,
    seq_lengths,
    live_counts,
    ln1_gain,
    ln1_shift,
    w_qkv,
    q_bias,
    v_bias,
    w_out,
    out_bias,
    ln2_gain,
    ln2_shift,
    w_up,
    up_bias,
    w_down,
    down_bias,
):
    forward_params = (
        lax.all_gather(ln1_gain, "shard", axis=0, tiled=True),
        lax.all_gather(ln1_shift, "shard", axis=0, tiled=True),
        lax.all_gather(w_qkv, "shard", axis=0, tiled=True),
        lax.all_gather(q_bias, "shard", axis=0, tiled=True),
        lax.all_gather(v_bias, "shard", axis=0, tiled=True),
        lax.all_gather(w_out, "shard", axis=0, tiled=True),
        lax.all_gather(out_bias, "shard", axis=0, tiled=True),
        lax.all_gather(ln2_gain, "shard", axis=0, tiled=True),
        lax.all_gather(ln2_shift, "shard", axis=0, tiled=True),
        lax.all_gather(w_up, "shard", axis=1, tiled=True),
        lax.all_gather(up_bias, "shard", axis=0, tiled=True),
        lax.all_gather(w_down, "shard", axis=0, tiled=True),
        lax.all_gather(down_bias, "shard", axis=0, tiled=True),
    )
    backward_params = (
        lax.all_gather(ln1_gain, "shard", axis=0, tiled=True),
        lax.all_gather(ln1_shift, "shard", axis=0, tiled=True),
        lax.all_gather(w_qkv, "shard", axis=0, tiled=True),
        lax.all_gather(q_bias, "shard", axis=0, tiled=True),
        lax.all_gather(v_bias, "shard", axis=0, tiled=True),
        lax.all_gather(w_out, "shard", axis=0, tiled=True),
        lax.all_gather(out_bias, "shard", axis=0, tiled=True),
        lax.all_gather(ln2_gain, "shard", axis=0, tiled=True),
        lax.all_gather(ln2_shift, "shard", axis=0, tiled=True),
        lax.all_gather(w_up, "shard", axis=1, tiled=True),
        lax.all_gather(up_bias, "shard", axis=0, tiled=True),
        lax.all_gather(w_down, "shard", axis=0, tiled=True),
        lax.all_gather(down_bias, "shard", axis=0, tiled=True),
    )
    result, grad_in, gradients = layer_pass(
        tokens_in, cotangent, seq_lengths[0], live_counts[0], forward_params, backward_params
    )
    (
        grad_gain_one,
        grad_shift_one,
        grad_wqkv,
        grad_bquery,
        grad_bvalue,
        grad_wout,
        grad_bout,
        grad_gain_two,
        grad_shift_two,
        grad_wup,
        grad_bup,
        grad_wdown,
        grad_bdown,
    ) = gradients
    owned = (
        lax.psum_scatter(grad_gain_one, "shard", scatter_dimension=0, tiled=True),
        lax.psum_scatter(grad_shift_one, "shard", scatter_dimension=0, tiled=True),
        lax.psum_scatter(grad_wqkv, "shard", scatter_dimension=0, tiled=True),
        lax.psum_scatter(grad_bquery, "shard", scatter_dimension=0, tiled=True),
        lax.psum_scatter(grad_bvalue, "shard", scatter_dimension=0, tiled=True),
        lax.psum_scatter(grad_wout, "shard", scatter_dimension=0, tiled=True),
        lax.psum_scatter(grad_bout, "shard", scatter_dimension=0, tiled=True),
        lax.psum_scatter(grad_gain_two, "shard", scatter_dimension=0, tiled=True),
        lax.psum_scatter(grad_shift_two, "shard", scatter_dimension=0, tiled=True),
        lax.psum_scatter(grad_wup, "shard", scatter_dimension=1, tiled=True),
        lax.psum_scatter(grad_bup, "shard", scatter_dimension=0, tiled=True),
        lax.psum_scatter(grad_wdown, "shard", scatter_dimension=0, tiled=True),
        lax.psum_scatter(grad_bdown, "shard", scatter_dimension=0, tiled=True),
    )
    (
        owned_gain_one,
        owned_shift_one,
        owned_wqkv,
        owned_bquery,
        owned_bvalue,
        owned_wout,
        owned_bout,
        owned_gain_two,
        owned_shift_two,
        owned_wup,
        owned_bup,
        owned_wdown,
        owned_bdown,
    ) = owned
    summed = lax.psum(
        (
            owned_gain_one,
            owned_shift_one,
            owned_wqkv,
            owned_bquery,
            owned_bvalue,
            owned_wout,
            owned_bout,
            owned_gain_two,
            owned_shift_two,
            owned_wup,
            owned_bup,
            owned_wdown,
            owned_bdown,
        ),
        "rep",
    )
    return (result, grad_in) + tuple(summed)


def solution(mesh):
    return jax.shard_map(
        local,
        mesh=mesh,
        in_specs=(
            P(("rep", "shard"), None),
            P(("rep", "shard"), None),
            P(("rep", "shard"), None),
            P(("rep", "shard")),
            P("shard"),
            P("shard"),
            P("shard", None),
            P("shard"),
            P("shard"),
            P("shard", None),
            P("shard"),
            P("shard"),
            P("shard"),
            P(None, "shard"),
            P("shard"),
            P("shard", None),
            P("shard"),
        ),
        out_specs=(
            P(("rep", "shard"), None),
            P(("rep", "shard"), None),
            P("shard"),
            P("shard"),
            P("shard", None),
            P("shard"),
            P("shard"),
            P("shard", None),
            P("shard"),
            P("shard"),
            P("shard"),
            P(None, "shard"),
            P("shard"),
            P("shard", None),
            P("shard"),
        ),
        check_vma=False,
    )
```

profile of v0, /device:TPU:1, one launch (start us, length us, event | category | flops | bytes accessed | tf_op | source)
XLA Modules:
  0.0 588.5 jit_solution(11918973068598742759)
XLA Ops:
  10.8 1.8 all-gather
  12.7 1.8 all-gather.1
  14.6 1.8 all-gather.2
  16.5 1.8 all-gather.3
  18.3 1.8 all-gather.4
  20.8 1.8 all-gather.5
  22.7 1.8 all-gather.6
  24.6 1.8 all-gather.7
  29.1 3.2 fusion.1
  32.4 0.9 copy.62
  33.3 0.9 copy.61
  34.2 0.9 copy.60
  35.1 1.9 fusion.11
  37.0 1.5 exponential_reduce_fusion
  39.1 1.6 convolution_convert_fusion.1
  40.8 1.9 fusion.91
  44.4 9.6 %all-gather.18.cloned.1.call-done = bf16[768,3072]{1,0:T(8,128)(2,1)} async-done(((bf16[768,1536]{1,0:T(8,128)(2,1)}), bf16[768,3072]{1,0:T(8,128)(2,1)}) %all-gather.18.cloned.1.call-update) | async-done | bytes 4718608 | tf_op jit(solution)/shard_map/all_gather | solution.py:212
  53.9 5.7 convolution_add_fusion.1
  59.7 11.3 %all-gather.20.cloned.1.call-done = bf16[3072,768]{1,0:T(8,128)(2,1)} async-done(((bf16[1536,768]{1,0:T(8,128)(2,1)}), bf16[3072,768]{1,0:T(8,128)(2,1)}) %all-gather.20.cloned.1.call-update) | async-done | bytes 4718608 | tf_op jit(solution)/shard_map/all_gather | solution.py:214
  71.0 6.9 %fusion.94 = (f32[3072]{0:T(1024)}, bf16[256,3072]{1,0:T(8,128)(2,1)S(1)}) fusion(f32[256,3072]{1,0:T(8,128)} %convolution_add_fusion.1, bf16[3072,768]{1,0:T(8,128)(2,1)} %all-gather.20.cloned.1.call-done, bf16[256,768]{1,0:T(8,128)(2,1)} %param.18, f32[256]{0:T(256)} %fusion.84), kind=kOutput, calls=%fused_computation.120 | convolution fusion | flops 1225061376 | bytes 9843712 | tf_op jit(solution)/shard_map/dot_general | solution.py:14
  78.0 2.2 multiply_reduce_fusion.1
  80.2 1.0 fusion.87
  81.2 0.9 copy-done
  82.0 1.9 fusion.57
  84.2 2.8 convolution_convert_fusion
  87.0 1.9 copy.64
  88.9 3.4 fusion.95
  92.3 6.0 %fusion.26 = bf16[12,64,256]{2,1,0:T(8,128)(2,1)} fusion(bf16[256,12,64]{0,2,1:T(8,128)(2,1)} %bitcast.52, f32[12,256,256]{1,2,0:T(8,128)} %fusion.95, f32[12,256,256]{1,2,0:T(8,128)S(1)} %get-tuple-element.56, f32[12,256]{1,0:T(8,128)} %copy-done.27, pred[256,256]{0,1:T(8,128)(4,1)} %fusion.55), kind=kOutput, calls=%fused_computation.31 | convolution fusion | flops 109513984 | bytes 7155712 | tf_op jit(solution)/shard_map/hqk,qhd->khd/dot_general | solution.py:18
  98.3 6.3 %fusion.90 = (f32[12,64]{1,0:T(8,128)}, bf16[256,12,64]{0,2,1:T(8,128)(2,1)}) fusion(bf16[256,12,64]{0,2,1:T(8,128)(2,1)} %bitcast.50, f32[12,256,256]{1,2,0:T(8,128)} %fusion.95, f32[12,256]{1,0:T(8,128)} %copy-done.27, f32[12,256,256]{1,2,0:T(8,128)S(1)} %get-tuple-element.56, pred[256,256]{0,1:T(8,128)(4,1)} %fusion.55), kind=kOutput, calls=%fused_computation.118 | convolution fusion | flops 109709824 | bytes 7158784 | tf_op jit(solution)/shard_map/hqk,khd->qhd/dot_general | solution.py:18
  104.6 2.6 fusion.89
  108.0 4.2 fusion.52
  112.2 1.8 copy-done.6
  114.1 7.6 %fusion.60 = f32[3072,768]{1,0:T(8,128)} fusion(bf16[256,768]{1,0:T(8,128)(2,1)} %param.18, f32[256]{0:T(256)S(1)} %copy-done.35, f32[256,3072]{1,0:T(8,128)S(1)} %copy-done.6), kind=kOutput, calls=%fused_computation.79 | convolution fusion | flops 1215627264 | bytes 12977152 | tf_op jit(solution)/shard_map/dot_general | solution.py:14
  121.7 1.0 copy-done.4
  123.4 5.4 fusion.46
  129.5 20.8 %reduce-scatter.11.cloned.1.call-done = f32[1536,768]{1,0:T(8,128)} async-done(((f32[3072,768]{1,0:T(8,128)}), f32[1536,768]{1,0:T(8,128)}) %reduce-scatter.11.cloned.1.call-update) | async-done | bytes 4718608 | tf_op jit(solution)/shard_map/reduce_scatter | solution.py:262
  150.3 20.7 %reduce-scatter.9.cloned.1.call-done = f32[768,1536]{1,0:T(8,128)} async-done(((f32[768,3072]{1,0:T(8,128)}), f32[768,1536]{1,0:T(8,128)}) %reduce-scatter.9.cloned.1.call-update) | async-done | bytes 4718608 | tf_op jit(solution)/shard_map/reduce_scatter | solution.py:260
  173.6 2.1 all-gather.8
  177.6 4.1 fusion.44
  181.7 4.2 all-reduce.11
  186.6 67.8 %all-reduce.9 = (f32[384]{0:T(512)}, f32[384]{0:T(512)}, f32[384]{0:T(512)}, f32[384]{0:T(512)}, f32[384]{0:T(512)}, /*index=5*/f32[384]{0:T(512)}, f32[384]{0:T(512)}, f32[1536]{0:T(1024)}, f32[384]{0:T(512)}) all-reduce(f32[384]{0:T(512)S(1)} %dynamic-slice.1, ...), channel_id=1, replica_groups=mesh['rep'=16,'shard'=2] {'rep'}, use_global_device_ids=true, to_apply=%region_15.16 | all-reduce | flops 4608 | bytes 36864 | tf_op jit(solution)/shard_map/psum | solution.py:280
  255.7 1.7 fusion.43
  257.4 6.4 %fusion.29 = bf16[256,768]{1,0:T(8,128)(2,1)} fusion(f32[256,768]{1,0:T(8,128)S(1)} %copy-done.4, bf16[3072,768]{1,0:T(8,128)(2,1)} %all-gather.20.cloned.1.call-done, f32[256]{0:T(256)} %fusion.84, f32[768]{0:T(1024)} %reshape.253, f32[256,3072]{1,0:T(8,128)} %convolution_add_fusion.1), kind=kOutput, calls=%fused_computation.34 | convolution fusion | flops 1215823872 | bytes 9048064 | tf_op jit(solution)/shard_map/dot_general | solution.py:14
  263.8 307.3 %all-reduce.14.cloned.1.call-done = (f32[384,2304]{1,0:T(8,128)}, f32[384,768]{1,0:T(8,128)}, f32[768,1536]{1,0:T(8,128)}, f32[1536,768]{1,0:T(8,128)}) async-done(((f32[384,2304]{1,0:T(8,128)}, f32[384,768]{1,0:T(8,128)}, f32[768,1536]{1,0:T(8,128)}, f32[1536,768]{1,0:T(8,128)}), (f32[384,2304]{1,0:T(8,128)}, f32[384,768]{1,0:T(8,128)}, f32[768,1536]{1,0:T(8,128)}, ...) | async-done | bytes 14155792 | tf_op jit(solution)/shard_map/psum | solution.py:280
  571.1 4.2 copy.77
  575.3 1.0 copy.78
  576.3 2.4 copy.79
  579.8 2.2 copy.80
  (182 shorter events, 17.2 us)
Async XLA Ops:
  7.2 3.6 copy-start.37
  7.2 5.5 copy-start.38
  7.2 7.3 %copy-start.39 = (bf16[384]{0:T(512)(128)(2,1)S(1)}, bf16[384]{0:T(512)(128)(2,1)}, u32[]{:S(2)}) copy-start(bf16[384]{0:T(512)(128)(2,1)} %param.24) | copy-start | bytes 2308
  7.2 9.2 %copy-start.40 = (bf16[384]{0:T(512)(128)(2,1)S(1)}, bf16[384]{0:T(512)(128)(2,1)}, u32[]{:S(2)}) copy-start(bf16[384]{0:T(512)(128)(2,1)} %param.25) | copy-start | bytes 2308
  7.2 11.1 %copy-start.41 = (bf16[384]{0:T(512)(128)(2,1)S(1)}, bf16[384]{0:T(512)(128)(2,1)}, u32[]{:S(2)}) copy-start(bf16[384]{0:T(512)(128)(2,1)} %param.27) | copy-start | bytes 2308
  7.2 21.8 %all-gather.14.cloned.1.call-start = ((), (), s32[]{:S(2)}) async-start(), calls=%async_computation.4 | async-start | bytes 5308416 | tf_op jit(solution)/shard_map/all_gather | solution.py:205
  8.0 12.8 %copy-start.42 = (bf16[384]{0:T(512)(128)(2,1)S(1)}, bf16[384]{0:T(512)(128)(2,1)}, u32[]{:S(2)}) copy-start(bf16[384]{0:T(512)(128)(2,1)} %param.28) | copy-start | bytes 2308
  8.0 14.7 %copy-start.43 = (bf16[384]{0:T(512)(128)(2,1)S(1)}, bf16[384]{0:T(512)(128)(2,1)}, u32[]{:S(2)}) copy-start(bf16[384]{0:T(512)(128)(2,1)} %param.29) | copy-start | bytes 2308
  8.0 16.6 %copy-start.36 = (bf16[1536]{0:T(1024)(128)(2,1)S(1)}, bf16[1536]{0:T(1024)(128)(2,1)}, u32[]{:S(2)}) copy-start(bf16[1536]{0:T(1024)(128)(2,1)} %param.31) | copy-start | bytes 9220
  8.0 19.0 %copy-start.46 = (s32[1,4]{1,0:T(1,128)S(1)}, s32[1,4]{1,0:T(1,128)}, u32[]{:S(2)}) copy-start(s32[1,4]{1,0:T(1,128)} %param.19) | copy-start | bytes 52
  8.0 19.9 %copy-start.5 = (bf16[256,768]{1,0:T(8,128)(2,1)S(1)}, bf16[256,768]{1,0:T(8,128)(2,1)}, u32[]{:S(2)}) copy-start(bf16[256,768]{1,0:T(8,128)(2,1)} %param.17) | copy-start | bytes 1179652
  8.0 32.7 %all-gather.16.cloned.1.call-start = ((), (), s32[]{:S(2)}) async-start(), calls=%async_computation.5 | async-start | bytes 1769472 | tf_op jit(solution)/shard_map/all_gather | solution.py:208
  8.8 45.2 %all-gather.18.cloned.1.call-start = ((), (), s32[]{:S(2)}) async-start(), calls=%async_computation.6 | async-start | bytes 7077888 | tf_op jit(solution)/shard_map/all_gather | solution.py:212
  9.5 61.5 %all-gather.20.cloned.1.call-start = ((), (), s32[]{:S(2)}) async-start(), calls=%async_computation.7 | async-start | bytes 7077888 | tf_op jit(solution)/shard_map/all_gather | solution.py:214
  10.1 118.8 %reduce-scatter.7.cloned.1.call-start = ((), (), s32[]{:S(2)}) async-start(), calls=%async_computation.9 | async-start | bytes 3538944 | tf_op jit(solution)/shard_map/reduce_scatter | solution.py:256
  35.1 4.0 copy-start.11
  35.1 4.0 copy-start.13
  71.0 6.9 %copy-start.3 = (f32[256,768]{1,0:T(8,128)S(1)}, f32[256,768]{1,0:T(8,128)}, u32[]{:S(2)}) copy-start(f32[256,768]{1,0:T(8,128)} %copy-done.2) | copy-start | bytes 2359300
  71.0 6.9 %copy-start.20 = (f32[256]{0:T(256)S(1)}, f32[256]{0:T(256)}, u32[]{:S(2)}) copy-start(f32[256]{0:T(256)} %copy-done.19) | copy-start | bytes 3076
  71.0 6.9 %copy-start.28 = (f32[256]{0:T(256)S(1)}, f32[256]{0:T(256)}, u32[]{:S(2)}) copy-start(f32[256]{0:T(256)} %add_rsqrt_fusion) | copy-start | bytes 3076
  71.0 6.9 %copy-start.45 = (bf16[768,3072]{1,0:T(8,128)(2,1)S(1)}, bf16[768,3072]{1,0:T(8,128)(2,1)}, u32[]{:S(2)}) copy-start(bf16[768,3072]{1,0:T(8,128)(2,1)} %all-gather.18.cloned.1.call-done) | copy-start | bytes 14155780
  77.9 2.2 copy-start.8
  77.9 2.2 copy-start.10
  78.0 2.2 copy-start.34
  78.0 4.1 copy-start.7
  84.0 45.5 %reduce-scatter.5.cloned.1.call-start = ((), (), s32[]{:S(2)}) async-start(), calls=%async_computation.8 | async-start | bytes 10616832 | tf_op jit(solution)/shard_map/reduce_scatter | solution.py:253
  104.6 3.4 copy-start.14
  104.6 3.4 copy-start.16
  104.6 3.4 copy-start.23
  104.6 3.4 copy-start.31
  112.2 1.9 copy-start.35
  112.2 38.1 %reduce-scatter.11.cloned.1.call-start = ((), (), s32[]{:S(2)}) async-start(), calls=%async_computation.11 | async-start | bytes 14155776 | tf_op jit(solution)/shard_map/reduce_scatter | solution.py:262
  121.7 49.3 %reduce-scatter.9.cloned.1.call-start = ((), (), s32[]{:S(2)}) async-start(), calls=%async_computation.10 | async-start | bytes 14155776 | tf_op jit(solution)/shard_map/reduce_scatter | solution.py:260
  128.8 442.3 %all-reduce.14.cloned.1.call-start = ((), (), s32[]{:S(2)}) async-start(), calls=%async_computation.12 | async-start | bytes 28311552 | tf_op jit(solution)/shard_map/psum | solution.py:280
  171.0 2.5 copy-start.44
  171.0 5.2 copy-start.33
  171.0 5.9 %copy-start.32 = (f32[12,64]{1,0:T(8,128)S(1)}, f32[12,64]{1,0:T(8,128)}, u32[]{:S(2)}) copy-start(f32[12,64]{1,0:T(8,128)} %get-tuple-element.52) | copy-start | bytes 9220
  171.0 6.6 %copy-start.15 = (bf16[12,64,256]{2,1,0:T(8,128)(2,1)S(1)}, bf16[12,64,256]{2,1,0:T(8,128)(2,1)}, u32[]{:S(2)}) copy-start(bf16[12,64,256]{2,1,0:T(8,128)(2,1)} %fusion.26) | copy-start | bytes 1179652
  171.0 6.6 %copy-start.17 = (bf16[256,12,64]{0,2,1:T(8,128)(2,1)S(1)}, bf16[256,12,64]{0,2,1:T(8,128)(2,1)}, u32[]{:S(2)}) copy-start(bf16[256,12,64]{0,2,1:T(8,128)(2,1)} %get-tuple-element.53) | copy-start | bytes 1179652
  171.0 6.5 %copy-start.24 = (f32[256]{0:T(256)S(1)}, f32[256]{0:T(256)}, u32[]{:S(2)}) copy-start(f32[256]{0:T(256)} %copy-done.22) | copy-start | bytes 3076
  177.6 4.1 copy-start.25
  177.6 4.1 copy-start.26
  177.6 78.1 %copy-start.1 = (f32[256,768]{1,0:T(8,128)S(1)}, f32[256,768]{1,0:T(8,128)}, u32[]{:S(2)}) copy-start(f32[256,768]{1,0:T(8,128)} %copy-done) | copy-start | bytes 2359300
  571.1 5.2 slice-start.2
  571.1 4.2 copy-start.12
  571.1 5.2 slice-start.3
  575.3 4.1 slice-start
  576.3 3.4 slice-start.1
  (13 other events, 14.9 us)
Sparse Core Ops, SparseCore 0:
  9.6 15.1 all-gather.13
  26.3 10.3 all-gather.15
  38.3 15.6 all-gather.17
  55.3 15.6 all-gather.19
  84.1 11.3 reduce-scatter.6
  112.3 17.0 reduce-scatter.4
  131.7 18.5 reduce-scatter.10
  152.6 18.3 reduce-scatter.8
  177.4 393.6 all-reduce.13
where the time goes:
time: 590 us; the launch traced here: 588 us
  waiting for transfers between devices  373 us (63%)
  blocking collectives  88.7 us (15%)
  matrix products  74.1 us (13%)
  local copies, waits for them, and re-layouts  26.8 us (5%)
  between operations  16.3 us (3%)
  other arithmetic  9.08 us (2%)
    psum x1, waiting for transfers between devices, local(): lax.psum((owned_gain_one, owned_shift_one, owned_wqkv, owned_bquery, owne...  307 us
    psum x1, blocking collectives, local(): lax.psum((owned_gain_one, owned_shift_one, owned_wqkv, owned_bquery, owne...  67.8 us
    dot_general x12, matrix products, matmul(): return jnp.dot(left, right, preferred_element_type=jnp.float32)  52.2 us
    dot_general x6, matrix products, contract(): return jnp.einsum(form, left, right, preferred_element_type=jnp.float32)  21.8 us
    reduce_scatter x1, waiting for transfers between devices, local(): lax.psum_scatter(grad_wdown, 'shard', scatter_dimension=0, tiled=True)  20.8 us
    reduce_scatter x1, waiting for transfers between devices, local(): lax.psum_scatter(grad_wup, 'shard', scatter_dimension=1, tiled=True)  20.7 us
    unnamed x127, local copies, waits for them, and re-layouts  19.4 us
  transfers between devices with their start and end apart: 9, of which 6 were waited for; matrix products, arithmetic and copies ran while one was open for 14% of the time, Pallas kernels for 0%

commit v1 on v0

--- a/solution.py
+++ b/solution.py
@@ -1,6 +1,11 @@
+import functools
+import math
+
 import jax
 import jax.numpy as jnp
 from jax import lax
+from jax.experimental import pallas as pl
+from jax.experimental.pallas import tpu as pltpu
 from jax.sharding import PartitionSpec as P
 
 HEAD_DIM = 64
@@ -180,7 +185,7 @@
     return (result, grad_in, gradients)
 
 
-def local(
+def plain_local(
     tokens_in,
     cotangent,
     seq_lengths,
@@ -298,7 +303,583 @@
     return (result, grad_in) + tuple(summed)
 
 
+def exchange(array, axis, distance, size):
+    return lax.ppermute(array, axis, [(i, i ^ distance) for i in range(size)])
+
+
+def cross(array, distances, size):
+    pairs = [
+        (2 * place + core, 2 * (place ^ distance) + core)
+        for place in range(size)
+        for core, distance in enumerate(distances)
+    ]
+    return lax.ppermute(array, ("rep", "shard"), pairs)
+
+
+def rep_sum(keep, send, order, size):
+    keep = keep + cross(send, order[0], size)
+    for distances in order[1:]:
+        count = keep.shape[0] // 2
+        keep = keep[:count] + cross(keep[count:], distances, size)
+    for distances in reversed(order[1:]):
+        keep = jnp.concatenate([keep, cross(keep, distances, size)], 0)
+    return keep, cross(keep, order[0], size)
+
+
+def small_sum(array, size):
+    distance = 1
+    while distance < size:
+        array = array + exchange(array, "rep", distance, size)
+        distance *= 2
+    return array
+
+
+def dot_nt(left, right):
+    return lax.dot_general(left, right, (((1,), (1,)), ((), ())), preferred_element_type=jnp.float32)
+
+
+def dot_tn(left, right):
+    return lax.dot_general(left, right, (((0,), (0,)), ((), ())), preferred_element_type=jnp.float32)
+
+
+def f32(array):
+    return array.astype(jnp.float32)
+
+
+def bf16(array):
+    return array.astype(jnp.bfloat16)
+
+
+def lanes(offset, size):
+    return pl.ds(pl.multiple_of(offset, 128), size)
+
+
+def call(kernel, outs, operands, scalars, scratch=(), flops=0):
+    return pl.pallas_call(
+        kernel,
+        out_shape=[jax.ShapeDtypeStruct(shape, dtype) for shape, dtype in outs],
+        in_specs=[pl.BlockSpec(memory_space=pltpu.SMEM)] * scalars
+        + [pl.BlockSpec(memory_space=pltpu.VMEM)] * (len(operands) - scalars),
+        out_specs=[pl.BlockSpec(memory_space=pltpu.VMEM)] * len(outs),
+        scratch_shapes=list(scratch),
+        compiler_params=pltpu.CompilerParams(vmem_limit_bytes=48 << 20),
+        cost_estimate=pl.CostEstimate(flops=flops, transcendentals=0, bytes_accessed=8 << 20),
+    )(*operands)
+
+
+def allowed_pairs(numbers, block, rows):
+    row = lax.broadcasted_iota(jnp.int32, (rows, rows), 0)
+    col = lax.broadcasted_iota(jnp.int32, (rows, rows), 1)
+    row_segment, col_segment = jnp.zeros_like(row), jnp.zeros_like(col)
+    bound = 0
+    last = numbers.shape[1] - 1
+    for i in range(last):
+        bound = bound + numbers[block, i]
+        row_segment = row_segment + (row >= bound).astype(jnp.int32)
+        col_segment = col_segment + (col >= bound).astype(jnp.int32)
+    same = (row_segment == col_segment) & (col <= row)
+    return same & ((col < numbers[block, last]) | (row == col))
+
+
+def head_probs(query, keys, allowed):
+    scores = dot_nt(query, keys) * HEAD_DIM ** (-0.5)
+    scores = jnp.where(allowed, scores, masked_score)
+    powers = jnp.exp(scores - jnp.max(scores, -1, keepdims=True))
+    return powers / jnp.sum(powers, -1, keepdims=True)
+
+
+def attention_forward(
+    place, numbers, tokens, tokens_other, w_own, w_other, v_own, v_other, hidden, qkv, context, normed
+):
+    core = place[2]
+    rows, width = tokens.shape
+    half = width // 2
+    for block, ref in enumerate((tokens, tokens_other)):
+        values = f32(ref[...])
+        center = values - jnp.mean(values, -1, keepdims=True)
+        inverse = lax.rsqrt(jnp.mean(center * center, -1, keepdims=True) + epsilon_norm)
+        normed[block * rows : (block + 1) * rows, :] = center * inverse
+    for side, ref in enumerate((v_own, v_other)):
+        offset = jnp.where(core == side, 0, half)
+        part = normed[:, lanes(offset, half)]
+        hidden[:, side * half : (side + 1) * half] = bf16(part * ref[0:1, :] + ref[1:2, :])
+    for part in range(3):
+        cut = lanes(part * width + core * half, half)
+        total = jnp.dot(hidden[:, :half], w_own[:, cut], preferred_element_type=jnp.float32)
+        total += jnp.dot(hidden[:, half:], w_other[:, cut], preferred_element_type=jnp.float32)
+        if part != 1:
+            row = 6 + part // 2
+            total += v_own[row : row + 1, :]
+        qkv[:, part * half : (part + 1) * half] = bf16(total)
+    pair = 2 * HEAD_DIM
+    low = lax.broadcasted_iota(jnp.int32, (rows, pair), 1) < HEAD_DIM
+    for block in range(2):
+        span = slice(block * rows, (block + 1) * rows)
+        allowed = allowed_pairs(numbers, block, rows)
+        for start in range(0, half, pair):
+            query = qkv[span, start : start + pair]
+            keys = qkv[span, half + start : half + start + pair]
+            value = qkv[span, 2 * half + start : 2 * half + start + pair]
+            zero = jnp.zeros_like(query)
+            found = []
+            for mine in (low, ~low):
+                probs = head_probs(jnp.where(mine, query, zero), keys, allowed)
+                found.append(jnp.dot(bf16(probs), value, preferred_element_type=jnp.float32))
+            context[span, start : start + pair] = bf16(jnp.where(low, *found))
+
+
+def attention_backward(place, numbers, grads, grads_other, w_out, qkv, grad_qkv, sums):
+    rows = grads.shape[0]
+    half = w_out.shape[0]
+    pair = 2 * HEAD_DIM
+    scale = HEAD_DIM ** (-0.5)
+    low = lax.broadcasted_iota(jnp.int32, (rows, pair), 1) < HEAD_DIM
+    sums[...] = jnp.zeros_like(sums)
+    for block, ref in enumerate((grads, grads_other)):
+        span = slice(block * rows, (block + 1) * rows)
+        allowed = allowed_pairs(numbers, block, rows)
+        grad_context = bf16(dot_nt(ref[...], w_out[...]))
+        for start in range(0, half, pair):
+            cut = slice(start, start + pair)
+            query = qkv[span, start : start + pair]
+            keys = qkv[span, half + start : half + start + pair]
+            value = qkv[span, 2 * half + start : 2 * half + start + pair]
+            above = grad_context[:, cut]
+            zero = jnp.zeros_like(query)
+            found = []
+            for mine in (low, ~low):
+                probs = head_probs(jnp.where(mine, query, zero), keys, allowed)
+                grad_probs = dot_nt(jnp.where(mine, above, zero), value)
+                delta = jnp.sum(probs * grad_probs, -1, keepdims=True)
+                grad_scores = bf16(probs * (grad_probs - delta) * scale)
+                found.append(
+                    (
+                        jnp.dot(grad_scores, keys, preferred_element_type=jnp.float32),
+                        dot_tn(grad_scores, query),
+                        dot_tn(bf16(probs), above),
+                    )
+                )
+            for part, (first, second) in enumerate(zip(*found)):
+                grad = jnp.where(low, first, second)
+                grad_qkv[span, part * half + start : part * half + start + pair] = bf16(grad)
+                if part != 1:
+                    row = part // 2
+                    sums[row : row + 1, cut] += jnp.sum(grad, 0, keepdims=True)
+
+
+def store_blocks(place, first, second, keep, send, start):
+    rows = keep.shape[1]
+    flip, low_role = place[0], place[1]
+    for i in range(first.shape[0] // rows):
+        span = slice(i * rows, (i + 1) * rows)
+        lower, upper = bf16(first[span]), bf16(second[span])
+        where = (start // rows + i) ^ low_role
+        keep[where] = jnp.where(flip == 0, lower, upper)
+        send[where] = jnp.where(flip == 0, upper, lower)
+
+
+def feed_piece(place, hidden, grad_out, w_up, up_bias, w_down, keep, send, act, grad_up, bias_sum):
+    upper = jnp.dot(hidden[...], w_up[...], preferred_element_type=jnp.float32) + f32(up_bias[...])
+    root = (2.0 / math.pi) ** 0.5
+    square = upper * upper
+    slope = jnp.tanh(root * (upper + 0.044715 * square * upper))
+    act[...] = bf16(0.5 * upper * (1.0 + slope))
+    derivative = 0.5 * (1.0 + slope) + 0.5 * upper * (1.0 - slope * slope) * root * (
+        1.0 + 3.0 * 0.044715 * square
+    )
+    grad = dot_nt(grad_out[...], w_down[...]) * derivative
+    bias_sum[...] = jnp.sum(grad, 0, keepdims=True)
+    grad_up[...] = bf16(grad)
+    size = act.shape[1]
+    part = size // 2
+    for start in range(0, size, part):
+        cut = slice(start, start + part)
+        store_blocks(
+            place,
+            dot_tn(act[:, cut], grad_out[...]),
+            dot_tn(hidden[:, cut], grad_up[...]),
+            keep,
+            send,
+            start,
+        )
+
+
+def middle_forward(
+    place,
+    numbers,
+    context,
+    context_other,
+    w_out,
+    w_out_other,
+    tokens,
+    tokens_other,
+    v_own,
+    v_other,
+    cot,
+    cot_other,
+    w_up,
+    up_bias,
+    w_down,
+    resid_out,
+    hidden,
+    grad_out,
+    keep,
+    send,
+    act,
+    grad_up,
+    bias_sum,
+    vectors,
+):
+    core = place[2]
+    rows, width = tokens.shape
+    half = width // 2
+    last = numbers.shape[1] - 1
+    vectors[:, lanes(core * half, half)] = v_own[...]
+    vectors[:, lanes((1 - core) * half, half)] = v_other[...]
+    for block, (token_ref, cot_ref) in enumerate(((tokens, cot), (tokens_other, cot_other))):
+        span = slice(block * rows, (block + 1) * rows)
+        out = jnp.dot(context[span, :], w_out[...], preferred_element_type=jnp.float32)
+        out += jnp.dot(context_other[span, :], w_out_other[...], preferred_element_type=jnp.float32)
+        resid = f32(token_ref[...]) + out + vectors[2:3, :]
+        if block == 0:
+            resid_out[...] = resid
+        center = resid - jnp.mean(resid, -1, keepdims=True)
+        inverse = lax.rsqrt(jnp.mean(center * center, -1, keepdims=True) + epsilon_norm)
+        hidden[span, :] = bf16(center * inverse * vectors[3:4, :] + vectors[4:5, :])
+        position = lax.broadcasted_iota(jnp.int32, (rows, width), 0)
+        live = position < numbers[block, last]
+        grad_out[span, :] = bf16(jnp.where(live, f32(cot_ref[...]), 0.0))
+    feed_piece(
+        place, hidden, grad_out, w_up, up_bias, w_down, keep, send, act, grad_up, bias_sum
+    )
+
+
+def attention_weights(
+    place,
+    hidden,
+    grad_qkv,
+    grad_qkv_other,
+    context,
+    grads,
+    grads_other,
+    w_own,
+    w_other,
+    keep,
+    send,
+    grad_own,
+    grad_other,
+):
+    core = place[2]
+    rows, width = grads.shape
+    half = width // 2
+    wide = 3 * half
+    rows_block = keep.shape[1]
+    left = hidden[:, :half]
+    first = dot_tn(left, grad_qkv[...])
+    second = dot_tn(hidden[:rows, :half], grad_qkv_other[rows:, :])
+    second += dot_tn(hidden[rows:, :half], grad_qkv_other[:rows, :])
+    third = dot_tn(context[:rows, :], grads[...]) + dot_tn(context[rows:, :], grads_other[...])
+    flip, low_role = place[0], place[1]
+    for i in range(half // rows_block):
+        span = slice(i * rows_block, (i + 1) * rows_block)
+        where = i ^ low_role
+        for cut, lower, upper in (
+            (slice(0, wide), first[span], second[span]),
+            (slice(wide, wide + half), third[span, :half], third[span, half:]),
+        ):
+            lower, upper = bf16(lower), bf16(upper)
+            keep[where, :, cut] = jnp.where(flip == 0, lower, upper)
+            send[where, :, cut] = jnp.where(flip == 0, upper, lower)
+    for side, ref in enumerate((w_own, w_other)):
+        target = lanes(jnp.where(core == side, 0, half), half)
+        total = jnp.zeros((2 * rows, half), jnp.float32)
+        for part in range(3):
+            cut = lanes(part * width + core * half, half)
+            total += dot_nt(grad_qkv[:, part * half : (part + 1) * half], ref[:, cut])
+        grad_own[:, target] = total[:rows]
+        grad_other[:, target] = total[rows:]
+
+
+def unpack_feed(own, other, place, before, hidden, piece):
+    count, rows, width = own.shape
+    kept = len(before)
+
+    def kernel(place_ref, own_ref, other_ref, *refs):
+        down_out, up_out = refs[kept:]
+        mine, theirs = f32(own_ref[0]), f32(other_ref[0])
+        down_out[...] = jnp.where(place_ref[0] == 0, mine, theirs)
+        up_out[...] = jnp.where(place_ref[0] == 0, theirs, mine)
+
+    block = pl.BlockSpec((1, rows, width), lambda i, place_ref: (i ^ place_ref[1], 0, 0))
+    return pl.pallas_call(
+        kernel,
+        out_shape=[
+            jax.ShapeDtypeStruct((hidden, width), jnp.float32),
+            jax.ShapeDtypeStruct((width, hidden), jnp.float32),
+        ],
+        grid_spec=pltpu.PrefetchScalarGridSpec(
+            num_scalar_prefetch=1,
+            grid=(count,),
+            in_specs=[block, block] + [pl.BlockSpec(memory_space=pl.ANY)] * kept,
+            out_specs=[
+                pl.BlockSpec((rows, width), lambda i, place_ref: (piece * count + i, 0)),
+                pl.BlockSpec((rows, width), lambda i, place_ref: (i, piece)),
+            ],
+        ),
+        input_output_aliases={3: 0, 4: 1} if kept else {},
+    )(place, own, other, *before)
+
+
+def unpack_attention(own, other, place):
+    count, rows, wide = own.shape
+    half = wide // 4
+
+    def kernel(place_ref, own_ref, other_ref, qkv_out, out_out):
+        mine, theirs = f32(own_ref[0]), f32(other_ref[0])
+        first = jnp.where(place_ref[0] == 0, mine, theirs)
+        second = jnp.where(place_ref[0] == 0, theirs, mine)
+        core = place_ref[2]
+        for part in range(3):
+            cut = slice(part * half, (part + 1) * half)
+            base = part * 2 * half
+            qkv_out[:, lanes(base + core * half, half)] = first[:, cut]
+            qkv_out[:, lanes(base + (1 - core) * half, half)] = second[:, cut]
+        out_out[:, :half] = first[:, 3 * half :]
+        out_out[:, half:] = second[:, 3 * half :]
+
+    block = pl.BlockSpec((1, rows, wide), lambda i, place_ref: (i ^ place_ref[1], 0, 0))
+    return pl.pallas_call(
+        kernel,
+        out_shape=[
+            jax.ShapeDtypeStruct((count * rows, 6 * half), jnp.float32),
+            jax.ShapeDtypeStruct((count * rows, 2 * half), jnp.float32),
+        ],
+        grid_spec=pltpu.PrefetchScalarGridSpec(
+            num_scalar_prefetch=1,
+            grid=(count,),
+            in_specs=[block, block],
+            out_specs=[
+                pl.BlockSpec((rows, 6 * half), lambda i, place_ref: (i, 0)),
+                pl.BlockSpec((rows, 2 * half), lambda i, place_ref: (i, 0)),
+            ],
+        ),
+    )(place, own, other)
+
+
+def pair_local(
+    tokens_in,
+    cotangent,
+    seq_lengths,
+    live_counts,
+    ln1_gain,
+    ln1_shift,
+    w_qkv,
+    q_bias,
+    v_bias,
+    w_out,
+    out_bias,
+    ln2_gain,
+    ln2_shift,
+    w_up,
+    up_bias,
+    w_down,
+    down_bias,
+    reps,
+):
+    core, rep = lax.axis_index("shard"), lax.axis_index("rep")
+    first = core == 0
+
+    def swap(array):
+        return exchange(array, "shard", 1, 2)
+
+    def natural(own, other):
+        return jnp.concatenate([jnp.where(first, own, other), jnp.where(first, other, own)], 1)
+
+    order = rep_order(reps)
+    role = 0
+    for distances in order:
+        distance = jnp.where(first, *distances)
+        role = 2 * role + (rep // distance) % 2
+    top = reps // 2
+    place = jnp.stack([role // top, role % top, core]).astype(jnp.int32)
+
+    rows, width = tokens_in.shape
+    half = width // 2
+    hidden = w_up.shape[1]
+    both = 2 * rows
+    wide = 3 * half
+    b, f = jnp.bfloat16, jnp.float32
+    w_other = swap(w_qkv)
+    tokens_other = swap(tokens_in)
+    small = (ln1_gain, ln1_shift, out_bias, ln2_gain, ln2_shift, down_bias, q_bias, v_bias)
+    row = lax.broadcasted_iota(jnp.int32, (len(small), half), 0)
+    v_own = sum(jnp.where(row == i, f32(v)[None], 0.0) for i, v in enumerate(small))
+    v_other = swap(v_own)
+    numbers = jnp.concatenate([seq_lengths, live_counts[:, None]], 1)
+    numbers = jnp.concatenate([numbers, swap(numbers)], 0)
+    w_out_other = swap(w_out)
+    cot_other = swap(cotangent)
+    hidden_one, qkv, context = call(
+        attention_forward,
+        [((both, width), b), ((both, wide), b), ((both, half), b)],
+        (place, numbers, tokens_in, tokens_other, w_qkv, w_other, v_own, v_other),
+        2,
+        [pltpu.VMEM((both, width), f)],
+        2 * both * width * wide,
+    )
+    context_other = swap(jnp.concatenate([context[rows:], context[:rows]], 0))
+    pieces = hidden // width
+    biases = up_bias[None]
+    block = 2 * width // reps
+    packed = ((top, block, width), b)
+    piece_outs = [packed, packed, ((both, width), b), ((both, width), b), ((1, width), f)]
+    feeds = []
+    flops = 8 * both * width * width
+    for i in range(pieces):
+        cut = slice(i * width, (i + 1) * width)
+        weights = (w_up[:, cut], biases[:, cut], w_down[cut])
+        if i == 0:
+            resid, hidden_two, grad_out_b, *outs = call(
+                middle_forward,
+                [((rows, width), f), ((both, width), b), ((both, width), b)] + piece_outs,
+                (
+                    place,
+                    numbers,
+                    context,
+                    context_other,
+                    w_out,
+                    w_out_other,
+                    tokens_in,
+                    tokens_other,
+                    v_own,
+                    v_other,
+                    cotangent,
+                    cot_other,
+                )
+                + weights,
+                2,
+                [pltpu.VMEM((8, width), f)],
+                flops,
+            )
+        else:
+            outs = call(
+                feed_piece, piece_outs, (place, hidden_two, grad_out_b) + weights, 1, (), flops
+            )
+        feeds.append(outs)
+    vectors = natural(v_own, v_other)
+    gain_one, gain_two, bias_down = vectors[0], vectors[3], vectors[5]
+    acts = [outs[2] for outs in feeds]
+    grad_ups = [outs[3] for outs in feeds]
+
+    def back(span):
+        return sum(
+            matmul(g[span], w_up[:, i * width : (i + 1) * width].T) for i, g in enumerate(grad_ups)
+        )
+
+    def ahead(span):
+        return sum(
+            matmul(a[span], w_down[i * width : (i + 1) * width]) for i, a in enumerate(acts)
+        )
+
+    mine, theirs = slice(0, rows), slice(rows, both)
+    live_col = f32(jnp.arange(rows, dtype=jnp.int32) < live_counts[0])[:, None]
+    grad_hidden_two = back(mine) + swap(back(theirs))
+    grad_out = f32(cotangent) * live_col
+    _, normed_two, inverse_two = norm_forward(resid, 1.0, 0.0)
+    grad_resid_norm, grad_gain_two, grad_shift_two = norm_backward(
+        grad_hidden_two, normed_two, inverse_two, gain_two
+    )
+    grad_resid = grad_out + grad_resid_norm
+    grad_resid_b = bf16(grad_resid)
+    grad_resid_other = swap(grad_resid_b)
+    grad_qkv, sums = call(
+        attention_backward,
+        [((both, wide), b), ((8, half), f)],
+        (place, numbers, grad_resid_b, grad_resid_other, w_out, qkv),
+        2,
+        (),
+        4 * both * width * half,
+    )
+    grad_qkv_other = swap(grad_qkv)
+    packed = ((top, 2 * half // reps, wide + half), b)
+    keep, send, grad_one, grad_one_other = call(
+        attention_weights,
+        [packed, packed, ((rows, width), f), ((rows, width), f)],
+        (
+            place,
+            hidden_one,
+            grad_qkv,
+            grad_qkv_other,
+            context,
+            grad_resid_b,
+            grad_resid_other,
+            w_qkv,
+            w_other,
+        ),
+        1,
+        (),
+        6 * both * width * wide // 2,
+    )
+    grad_hidden_one = grad_one + swap(grad_one_other)
+    _, normed_one, inverse_one = norm_forward(f32(tokens_in), 1.0, 0.0)
+    grad_in_norm, grad_gain_one, grad_shift_one = norm_backward(
+        grad_hidden_one, normed_one, inverse_one, gain_one
+    )
+    grad_in = bf16(grad_resid + grad_in_norm)
+    result = bf16((resid + ahead(mine) + swap(ahead(theirs)) + bias_down) * live_col)
+    sums_feed = ()
+    for i, outs in enumerate(feeds):
+        halves = rep_sum(outs[0], outs[1], order, reps)
+        sums_feed = unpack_feed(*halves, place, sums_feed, hidden, i)
+    grad_wdown, grad_wup = sums_feed
+    grad_wqkv, grad_wout = unpack_attention(*rep_sum(keep, send, order, reps), place)
+    wide_sums = (
+        grad_gain_one,
+        grad_shift_one,
+        jnp.sum(grad_resid, 0),
+        grad_gain_two,
+        grad_shift_two,
+        jnp.sum(grad_out, 0),
+    )
+    row = lax.broadcasted_iota(jnp.int32, (len(wide_sums), width), 0)
+    table = sum(jnp.where(row == i, v[None], 0.0) for i, v in enumerate(wide_sums))
+    own = jnp.where(first, table[:, :half], table[:, half:])
+    other = jnp.where(first, table[:, half:], table[:, :half])
+    up_sums = jnp.concatenate([outs[4].reshape(-1, half) for outs in feeds], 0)
+    pack = small_sum(jnp.concatenate([own + swap(other), sums[:2], up_sums], 0), reps)
+    return (
+        result,
+        grad_in,
+        pack[0],
+        pack[1],
+        grad_wqkv,
+        pack[6],
+        pack[7],
+        grad_wout,
+        pack[2],
+        pack[3],
+        pack[4],
+        grad_wup,
+        pack[8:].reshape(-1),
+        grad_wdown,
+        pack[5],
+    )
+
+
+def rep_order(reps):
+    line = [(1 << i, 1 << i) for i in range(2, reps.bit_length() - 1)]
+    return [(1, 2), (2, 1)] + line
+
+
+def pair_fits(mesh):
+    reps = mesh.shape["rep"]
+    return mesh.shape["shard"] == 2 and 4 <= reps <= 16 and reps & (reps - 1) == 0
+
+
 def solution(mesh):
+    local = plain_local
+    if pair_fits(mesh):
+        local = functools.partial(pair_local, reps=mesh.shape["rep"])
     return jax.shard_map(
         local,
         mesh=mesh,

time: 590 us -> 248 us (0.42)
  waiting for transfers between devices: 373 us -> 104 us
  blocking collectives: 88.7 us -> 0 us
  matrix products: 74.1 us -> 10.6 us
  Pallas kernels: 0 us -> 53.3 us
  starting transfers between devices: 0.54 us -> 46 us
  between operations: 16.3 us -> 2.21 us
  local copies, waits for them, and re-layouts: 26.8 us -> 14.1 us
  other arithmetic: 9.08 us -> 16.7 us
    psum x1 -> x0, waiting for transfers between devices: 307 us -> none  [local(): lax.psum((owned_gain_one, owned_shift_one, owned_wqkv, owned_bquery, owne...]
    ppermute x0 -> x41, waiting for transfers between devices: none -> 104 us  [the longest x24 64.7 us: cross(): return lax.ppermute(array, ('rep', 'shard'), pairs)]
    psum x1 -> x0, blocking collectives: 67.8 us -> none  [local(): lax.psum((owned_gain_one, owned_shift_one, owned_wqkv, owned_bquery, owne...]
    pallas_call x0 -> x8, Pallas kernels: none -> 53.3 us  [the longest x5 32.1 us: call(): pl.pallas_call(kernel, out_shape=[jax.ShapeDtypeStruct(shape, dtype) for...]
    ppermute x0 -> x41, starting transfers between devices: none -> 46 us  [the longest x24 29.2 us: cross(): return lax.ppermute(array, ('rep', 'shard'), pairs)]
    reduce_scatter x4 -> x0, waiting for transfers between devices: 42.1 us -> none  [the longest x1 20.8 us: local(): lax.psum_scatter(grad_wdown, 'shard', scatter_dimension=0, tiled=True)]
    dot_general x12 -> x8, matrix products: 52.2 us -> 10.6 us  [matmul(): return jnp.dot(left, right, preferred_element_type=jnp.float32)]
    dot_general x6 -> x0, matrix products: 21.8 us -> none  [contract(): return jnp.einsum(form, left, right, preferred_element_type=jnp.float32)]
  transfers between devices with their start and end apart: 9 -> 41, of which waited for: 6 -> 15; matrix products, arithmetic and copies ran while one was open for 14% -> 12% of each run, Pallas kernels for 0% -> 14%
where the time goes in v1:
time: 248 us; the launch traced here: 247 us
  waiting for transfers between devices  104 us (42%)
  Pallas kernels  53.3 us (21%)
  starting transfers between devices  46 us (19%)
  other arithmetic  16.7 us (7%)
  local copies, waits for them, and re-layouts  14.1 us (6%)
  matrix products  10.6 us (4%)
    ppermute x24, waiting for transfers between devices, cross(): return lax.ppermute(array, ('rep', 'shard'), pairs)  64.7 us
    ppermute x17, waiting for transfers between devices, exchange(): return lax.ppermute(array, axis, [(i, i ^ distance) for i in range(size)])  39.5 us
    pallas_call x5, Pallas kernels, call(): pl.pallas_call(kernel, out_shape=[jax.ShapeDtypeStruct(shape, dtype) for...  32.1 us
    ppermute x24, starting transfers between devices, cross(): return lax.ppermute(array, ('rep', 'shard'), pairs)  29.2 us
    ppermute x17, starting transfers between devices, exchange(): return lax.ppermute(array, axis, [(i, i ^ distance) for i in range(size)])  16.8 us
    pallas_call x2, Pallas kernels, unpack_feed(): pl.pallas_call(kernel, out_shape=[jax.ShapeDtypeStruct((hidden, width), j...  14.2 us
    dot_general x8, matrix products, matmul(): return jnp.dot(left, right, preferred_element_type=jnp.float32)  10.6 us
    unnamed x108, local copies, waits for them, and re-layouts  7.12 us
  transfers between devices with their start and end apart: 41, of which 15 were waited for; matrix products, arithmetic and copies ran while one was open for 12% of the time, Pallas kernels for 14%

profile of v1, /device:TPU:1, one launch (start us, length us, event | category | flops | bytes accessed | tf_op | source)
XLA Modules:
  0.0 247.1 jit_solution(8687048801925337170)
XLA Ops:
  9.6 4.7 %fusion.42 = (bf16[768,768]{1,0:T(8,128)(2,1)}, bf16[768,768]{1,0:T(8,128)(2,1)}, bf16[768,768]{1,0:T(8,128)(2,1)}, bf16[768,768]{1,0:T(8,128)(2,1)}) fusion(bf16[1536,768]{1,0:T(8,128)(2,1)} %param.32, bf16[768,1536]{1,0:T(8,128)(2,1)} %param.30), kind=kLoop, calls=%fused_computation.119 | loop fusion | bytes 9437184 | tf_op jit(solution)/shard_map/slice | solution.py:740
  15.0 1.2 copy-done.28
  16.2 5.5 %shard_map.280 = (bf16[512,768]{1,0:T(8,128)(2,1)S(1)}, bf16[512,1152]{1,0:T(8,128)(2,1)S(1)}, bf16[512,384]{1,0:T(8,128)(2,1)S(1)}) custom-call(s32[3]{0:T(128)S(1)} %pad_add_fusion.1.place.place_ref, s32[2,5]{1,0:T(2,128)S(1)} %pad_add_fusion.numbers, bf16[256,768]{1,0:T(8,128)(2,1)S(1)} %copy-done, ...), custom_call_target="tpu_custom_call" | custom-call | flops 905969664 | bytes 8388608 | tf_op jit(solution)/shard_map/pallas_call | solution.py:358
  25.5 7.7 %shard_map.281 = (f32[256,768]{1,0:T(8,128)S(1)}, bf16[512,768]{1,0:T(8,128)(2,1)S(1)}, bf16[512,768]{1,0:T(8,128)(2,1)S(1)}, bf16[8,96,768]{2,1,0:T(8,128)(2,1)...) custom-call(s32[3]{0:T(128)S(1)} %pad_add_fusion.1.place.place_ref, ...), custom_call_target="tpu_custom_call" | custom-call | flops 2415919104 | bytes 8388608 | tf_op jit(solution)/shard_map/pallas_call | solution.py:358
  33.2 5.0 %shard_map.282 = (bf16[8,96,768]{2,1,0:T(8,128)(2,1)S(1)}, bf16[8,96,768]{2,1,0:T(8,128)(2,1)S(1)}, bf16[512,768]{1,0:T(8,128)(2,1)S(1)}, bf16[512,768]{1,0:T(8,128)(2,1)S(1)}, f32[1,768]{1,0:T(1,128)S(1)}) custom-call(s32[3]{0:T(128)S(1)} %pad_add_fusion.1.place.place_ref, bf16[512,768]{1,0:T(8,128)(2,1)S(1)} %get-tuple-element.46.hidden, ...), custom_call_target="tpu_custom_call" | custom-call | flops 2415919104 | bytes 8388608 | tf_op jit(solution)/shard_map/pallas_call | solution.py:358
  39.9 1.4 convolution_add_fusion
  42.0 2.0 fusion.22
  44.2 2.0 multiply_reduce_fusion
  48.4 2.5 %collective-permute-start.25 = (bf16[8,96,768]{2,1,0:T(8,128)(2,1)S(1)}, bf16[8,96,768]{2,1,0:T(8,128)(2,1)S(1)}, u32[]{:S(2)}, u32[]{:S(2)}) collective-permute-start(bf16[8,96,768]{2,1,0:T(8,128)(2,1)S(1)} %copy-done.16), channel_id=1, source_target_pairs={{0,2},{1,5},{2,0},{3,7},{4,6},{5,1},{6,4},{7,3},{8,10},{9,13},{10,... | collective-permute-start | bytes 3538952 | tf_op jit(solution)/shard_map/ppermute | solution.py:316
  51.1 7.8 %shard_map.283 = (bf16[512,1152]{1,0:T(8,128)(2,1)S(1)}, f32[8,384]{1,0:T(8,128)S(1)}) custom-call(s32[3]{0:T(128)S(1)} %pad_add_fusion.1.place.place_ref, s32[2,5]{1,0:T(2,128)S(1)} %pad_add_fusion.numbers, bf16[256,768]{1,0:T(8,128)(2,1)S(1)} %convert_element_type.58.grads, bf16[256,768]{1,0:T(8,128)(2,1)S(1)} %collective-permute-done.9.grads_other, ...), custom_call_target="tpu_custom_call" | custom-call | flops 603979776 | bytes 8388608 | tf_op jit(solution)/shard_map/pallas_call | solution.py:358
  61.3 3.5 %collective-permute-done.25 = bf16[8,96,768]{2,1,0:T(8,128)(2,1)S(1)} collective-permute-done((bf16[8,96,768]{2,1,0:T(8,128)(2,1)S(1)}, bf16[8,96,768]{2,1,0:T(8,128)(2,1)S(1)}, u32[]{:S(2)}, u32[]{:S(2)}) %collective-permute-start.25) | collective-permute-done | bytes 1179680 | tf_op jit(solution)/shard_map/ppermute | solution.py:316
  65.2 1.5 collective-permute-start.26
  67.3 16.5 %collective-permute-done.33 = bf16[8,96,768]{2,1,0:T(8,128)(2,1)S(1)} collective-permute-done((bf16[8,96,768]{2,1,0:T(8,128)(2,1)S(1)}, bf16[8,96,768]{2,1,0:T(8,128)(2,1)S(1)}, u32[]{:S(2)}, u32[]{:S(2)}) %collective-permute-start.33) | collective-permute-done | bytes 1179680 | tf_op jit(solution)/shard_map/ppermute | solution.py:316
  84.2 1.5 collective-permute-start.34
  86.7 6.2 %shard_map.284 = (bf16[8,48,1536]{2,1,0:T(8,128)(2,1)S(1)}, bf16[8,48,1536]{2,1,0:T(8,128)(2,1)S(1)}, f32[256,768]{1,0:T(8,128)S(1)}, f32[256,768]{1,0:T(8,128)S(1)}) custom-call(s32[3]{0:T(128)S(1)} %pad_add_fusion.1.place.place_ref, bf16[512,768]{1,0:T(8,128)(2,1)S(1)} %copy-done.8, bf16[512,1152]{1,0:T(8,128)(2,1)} %copy-done.4, ...), custom_call_target="tpu_custom_call" | custom-call | flops 1358954496 | bytes 8388608 | tf_op jit(solution)/shard_map/pallas_call | solution.py:358
  92.9 1.3 collective-permute-start.17
  94.8 1.4 collective-permute-start.27
  96.5 1.4 convolution_add_fusion.2
  97.9 3.9 %collective-permute-done.27 = bf16[2,96,768]{2,1,0:T(8,128)(2,1)S(1)} collective-permute-done((bf16[2,96,768]{2,1,0:T(8,128)(2,1)S(1)}, bf16[2,96,768]{2,1,0:T(8,128)(2,1)S(1)}, u32[]{:S(2)}, u32[]{:S(2)}) %collective-permute-start.27) | collective-permute-done | bytes 294944 | tf_op jit(solution)/shard_map/ppermute | solution.py:316
  101.9 2.4 collective-permute-start.28
  104.3 4.0 %collective-permute-done.17 = bf16[8,48,1536]{2,1,0:T(8,128)(2,1)S(1)} collective-permute-done((bf16[8,48,1536]{2,1,0:T(8,128)(2,1)S(1)}, bf16[8,48,1536]{2,1,0:T(8,128)(2,1)S(1)}, u32[]{:S(2)}, u32[]{:S(2)}) %collective-permute-start.17) | collective-permute-done | bytes 1179680 | tf_op jit(solution)/shard_map/ppermute | solution.py:316
  109.8 1.9 collective-permute-start.36
  111.7 1.6 collective-permute-start.29
  113.3 9.6 %collective-permute-done.36 = bf16[1,96,768]{2,1,0:T(8,128)(2,1)S(1)} collective-permute-done((bf16[1,96,768]{2,1,0:T(8,128)(2,1)S(1)}, bf16[1,96,768]{2,1,0:T(8,128)(2,1)S(1)}, u32[]{:S(2)}, u32[]{:S(2)}) %collective-permute-start.36) | collective-permute-done | bytes 147488 | tf_op jit(solution)/shard_map/ppermute | solution.py:316
  123.1 1.9 collective-permute-start.19
  125.0 1.4 fusion.28
  126.5 7.9 %collective-permute-start.7 = (f32[256,768]{1,0:T(8,128)}, f32[256,768]{1,0:T(8,128)S(1)}, u32[]{:S(2)}, u32[]{:S(2)}) collective-permute-start(f32[256,768]{1,0:T(8,128)} %convolution_add_fusion.2), channel_id=1, source_target_pairs={{0,1},{1,0},{2,3},{3,2},{4,5},{5,4},{6,7},{7,6},{8,9},{9,8},{10,11... | collective-permute-start | bytes 2359304 | tf_op jit(solution)/shard_map/ppermute | solution.py:307
  134.5 1.5 collective-permute-start.38
  137.7 2.0 collective-permute-start.20
  139.7 7.0 %collective-permute-done.30 = bf16[2,96,768]{2,1,0:T(8,128)(2,1)S(1)} collective-permute-done((bf16[2,96,768]{2,1,0:T(8,128)(2,1)S(1)}, bf16[2,96,768]{2,1,0:T(8,128)(2,1)S(1)}, u32[]{:S(2)}, u32[]{:S(2)}) %collective-permute-start.30) | collective-permute-done | bytes 294944 | tf_op jit(solution)/shard_map/ppermute | solution.py:316
  146.8 6.2 %collective-permute-done.38 = bf16[2,96,768]{2,1,0:T(8,128)(2,1)S(1)} collective-permute-done((bf16[2,96,768]{2,1,0:T(8,128)(2,1)S(1)}, bf16[2,96,768]{2,1,0:T(8,128)(2,1)S(1)}, u32[]{:S(2)}, u32[]{:S(2)}) %collective-permute-start.38) | collective-permute-done | bytes 294944 | tf_op jit(solution)/shard_map/ppermute | solution.py:316
  154.3 5.1 %collective-permute-done.21 = bf16[1,48,1536]{2,1,0:T(8,128)(2,1)S(1)} collective-permute-done((bf16[1,48,1536]{2,1,0:T(8,128)(2,1)S(1)}, bf16[1,48,1536]{2,1,0:T(8,128)(2,1)S(1)}, u32[]{:S(2)}, u32[]{:S(2)}) %collective-permute-start.21) | collective-permute-done | bytes 147488 | tf_op jit(solution)/shard_map/ppermute | solution.py:316
  159.6 3.6 %collective-permute-start.12 = (f32[6,384]{1,0:T(8,128)S(1)}, f32[6,384]{1,0:T(8,128)S(1)}, u32[]{:S(2)}, u32[]{:S(2)}) collective-permute-start(f32[6,384]{1,0:T(8,128)S(1)} %slice_select_fusion), channel_id=1, source_target_pairs={{0,1},{1,0},{2,3},{3,2},{4,5},{5,4},{6,7},{7,6},{8,9},{9,8},{10,11... | collective-permute-start | bytes 27656 | tf_op jit(solution)/shard_map/ppermute | solution.py:307
  163.2 2.1 collective-permute-done.22
  165.3 5.3 %collective-permute-start.23 = (bf16[4,48,1536]{2,1,0:T(8,128)(2,1)S(1)}, bf16[4,48,1536]{2,1,0:T(8,128)(2,1)S(1)}, u32[]{:S(2)}, u32[]{:S(2)}) collective-permute-start(bf16[4,48,1536]{2,1,0:T(8,128)(2,1)S(1)} %pad_maximum_fusion.3), channel_id=1, source_target_pairs={{0,4},{1,3},{2,6},{3,1},{4,0},{5,7},{6,2},{7,5},{8,12},{9,11},{10,... | collective-permute-start | bytes 1769480 | tf_op jit(solution)/shard_map/ppermute | solution.py:316
  170.9 1.0 collective-permute-start.32
  171.9 1.1 pad_maximum_fusion.2.own_ref
  173.5 6.3 %collective-permute-done.23 = bf16[4,48,1536]{2,1,0:T(8,128)(2,1)S(1)} collective-permute-done((bf16[4,48,1536]{2,1,0:T(8,128)(2,1)S(1)}, bf16[4,48,1536]{2,1,0:T(8,128)(2,1)S(1)}, u32[]{:S(2)}, u32[]{:S(2)}) %collective-permute-start.23) | collective-permute-done | bytes 589856 | tf_op jit(solution)/shard_map/ppermute | solution.py:316
  180.0 1.1 collective-permute-start.24
  181.2 1.3 fusion.5
  183.0 35.1 %collective-permute-done.14 = f32[12,384]{1,0:T(8,128)S(1)} collective-permute-done((f32[12,384]{1,0:T(8,128)S(1)}, f32[12,384]{1,0:T(8,128)S(1)}, u32[]{:S(2)}, u32[]{:S(2)}) %collective-permute-start.14) | collective-permute-done | bytes 18464 | tf_op jit(solution)/shard_map/ppermute | solution.py:307
  218.2 2.6 %collective-permute-done.15 = f32[12,384]{1,0:T(8,128)S(1)} collective-permute-done((f32[12,384]{1,0:T(8,128)S(1)}, f32[12,384]{1,0:T(8,128)S(1)}, u32[]{:S(2)}, u32[]{:S(2)}) %collective-permute-start.15) | collective-permute-done | bytes 18464 | tf_op jit(solution)/shard_map/ppermute | solution.py:307
  220.8 1.1 collective-permute-start.16
  221.9 1.1 fusion.15
  223.0 1.6 collective-permute-done.16
  225.8 7.1 %shard_map.286 = (f32[1536,768]{1,0:T(8,128)}, f32[768,1536]{1,0:T(8,128)}) custom-call(s32[3]{0:T(128)} %copy-done.14, bf16[8,96,768]{2,1,0:T(8,128)(2,1)} %pad_maximum_fusion.2.own_ref, bf16[8,96,768]{2,1,0:T(8,128)(2,1)} %collective-permute-done.40.other_ref), custom_call_target="tpu_custom_call" | custom-call | tf_op jit(solution)/shard_map/pallas_call | solution.py:614
  232.9 7.1 %shard_map.287 = (f32[1536,768]{1,0:T(8,128)}, f32[768,1536]{1,0:T(8,128)}) custom-call(s32[3]{0:T(128)} %copy-done.14, bf16[8,96,768]{2,1,0:T(8,128)(2,1)} %copy-done.31, bf16[8,96,768]{2,1,0:T(8,128)(2,1)} %collective-permute-done.32.other_ref, f32[1536,768]{1,0:T(8,128)} %get-tuple-element.67.refs_0_, ...), custom_call_target="tpu_custom_call", output_to_operand_aliasing={{0}: (3, {}), {1}: (4, {})} | custom-call | tf_op jit(solution)/shard_map/pallas_call | solution.py:614
  240.0 7.1 %shard_map.285 = (f32[384,2304]{1,0:T(8,128)}, f32[384,768]{1,0:T(8,128)}) custom-call(s32[3]{0:T(128)} %copy-done.14, bf16[8,48,1536]{2,1,0:T(8,128)(2,1)} %copy-done.32, bf16[8,48,1536]{2,1,0:T(8,128)(2,1)} %collective-permute-done.24.other_ref), custom_call_target="tpu_custom_call" | custom-call | tf_op jit(solution)/shard_map/pallas_call | solution.py:651
  (247 shorter events, 31.0 us)
Async XLA Ops:
  0.6 14.3 %collective-permute-start.2 = (bf16[384,2304]{1,0:T(8,128)(2,1)}, bf16[384,2304]{1,0:T(8,128)(2,1)S(1)}, u32[]{:S(2)}, u32[]{:S(2)}) collective-permute-start(bf16[384,2304]{1,0:T(8,128)(2,1)} %w_own.3), channel_id=1, source_target_pairs={{0,1},{1,0},{2,3},{3,2},{4,5},{5,4},{6,7},{7,6},{8,9},{9,8},{10,11... | collective-permute-start | bytes 5308424 | tf_op jit(solution)/shard_map/ppermute | solution.py:307
  2.1 12.3 %collective-permute-start = (s32[1,5]{1,0:T(1,128)S(1)}, s32[1,5]{1,0:T(1,128)S(1)}, u32[]{:S(2)}, u32[]{:S(2)}) collective-permute-start(s32[1,5]{1,0:T(1,128)S(1)} %pad_add_fusion.2), channel_id=1, source_target_pairs={{0,1},{1,0},{2,3},{3,2},{4,5},{5,4},{6,7},{7,6},{8,9},{9,8},{10,11... | collective-permute-start | bytes 68 | tf_op jit(solution)/shard_map/ppermute | solution.py:307
  8.2 6.8 %collective-permute-start.3 = (f32[8,384]{1,0:T(8,128)S(1)}, f32[8,384]{1,0:T(8,128)S(1)}, u32[]{:S(2)}, u32[]{:S(2)}) collective-permute-start(f32[8,384]{1,0:T(8,128)S(1)} %select_add_fusion.2.v_own), channel_id=1, source_target_pairs={{0,1},{1,0},{2,3},{3,2},{4,5},{5,4},{6,7},{7,6},{8,9},{9,8},{10,11... | collective-permute-start | bytes 36872 | tf_op jit(solution)/shard_map/ppermute | solution.py:307
  8.3 15.3 %collective-permute-start.6 = (bf16[256,768]{1,0:T(8,128)(2,1)}, bf16[256,768]{1,0:T(8,128)(2,1)S(1)}, u32[]{:S(2)}, u32[]{:S(2)}) collective-permute-start(bf16[256,768]{1,0:T(8,128)(2,1)} %cot.1), channel_id=1, source_target_pairs={{0,1},{1,0},{2,3},{3,2},{4,5},{5,4},{6,7},{7,6},{8,9},{9,8},{10,11... | collective-permute-start | bytes 1179656 | tf_op jit(solution)/shard_map/ppermute | solution.py:307
  8.8 6.2 %collective-permute-start.1 = (bf16[256,768]{1,0:T(8,128)(2,1)}, bf16[256,768]{1,0:T(8,128)(2,1)S(1)}, u32[]{:S(2)}, u32[]{:S(2)}) collective-permute-start(bf16[256,768]{1,0:T(8,128)(2,1)} %tokens.3), channel_id=1, source_target_pairs={{0,1},{1,0},{2,3},{3,2},{4,5},{5,4},{6,7},{7,6},{8,9},{9,8},{10,11... | collective-permute-start | bytes 1179656 | tf_op jit(solution)/shard_map/ppermute | solution.py:307
  9.6 77.1 %copy-start.14 = (s32[3]{0:T(128)}, s32[3]{0:T(128)S(1)}, u32[]{:S(2)}) copy-start(s32[3]{0:T(128)S(1)} %pad_add_fusion.1.place.place_ref) | copy-start | bytes 40
  14.4 10.0 %collective-permute-start.5 = (bf16[384,768]{1,0:T(8,128)(2,1)S(1)}, bf16[384,768]{1,0:T(8,128)(2,1)S(1)}, u32[]{:S(2)}, u32[]{:S(2)}) collective-permute-start(bf16[384,768]{1,0:T(8,128)(2,1)S(1)} %copy-done.9), channel_id=1, source_target_pairs={{0,1},{1,0},{2,3},{3,2},{4,5},{5,4},{6,7},{7,6},{8,9},{9,8},{10,11... | collective-permute-start | bytes 1769480 | tf_op jit(solution)/shard_map/ppermute | solution.py:307
  22.7 1.8 collective-permute-start.4
  22.9 23.3 %copy-start.44 = (f32[256]{0:T(256)}, f32[256]{0:T(256)S(1)}, u32[]{:S(2)}) copy-start(f32[256]{0:T(256)S(1)} %compare_convert_fusion) | copy-start | bytes 3076
  41.3 2.7 %collective-permute-start.8 = (f32[256,768]{1,0:T(8,128)}, f32[256,768]{1,0:T(8,128)}, u32[]{:S(2)}, u32[]{:S(2)}) collective-permute-start(f32[256,768]{1,0:T(8,128)} %convolution_add_fusion), channel_id=1, source_target_pairs={{0,1},{1,0},{2,3},{3,2},{4,5},{5,4},{6,7},{7,6},{8,9},{9,8},{10,11... | collective-permute-start | bytes 2359304 | tf_op jit(solution)/shard_map/ppermute | solution.py:307
  48.2 2.9 %collective-permute-start.9 = (bf16[256,768]{1,0:T(8,128)(2,1)S(1)}, bf16[256,768]{1,0:T(8,128)(2,1)S(1)}, u32[]{:S(2)}, u32[]{:S(2)}) collective-permute-start(bf16[256,768]{1,0:T(8,128)(2,1)S(1)} %convert_element_type.58.grads), channel_id=1, source_target_pairs={{0,1},{1,0},{2,3},{3,2},{4,5},{5,4},{6,7},{7,6},{8,9},{9,8},{10,11... | collective-permute-start | bytes 1179656 | tf_op jit(solution)/shard_map/ppermute | solution.py:307
  48.4 16.4 %collective-permute-start.25 = (bf16[8,96,768]{2,1,0:T(8,128)(2,1)S(1)}, bf16[8,96,768]{2,1,0:T(8,128)(2,1)S(1)}, u32[]{:S(2)}, u32[]{:S(2)}) collective-permute-start(bf16[8,96,768]{2,1,0:T(8,128)(2,1)S(1)} %copy-done.16), channel_id=1, source_target_pairs={{0,2},{1,5},{2,0},{3,7},{4,6},{5,1},{6,4},{7,3},{8,10},{9,13},{10,... | collective-permute-start | bytes 3538952 | tf_op jit(solution)/shard_map/ppermute | solution.py:316
  51.0 32.8 %collective-permute-start.33 = (bf16[8,96,768]{2,1,0:T(8,128)(2,1)S(1)}, bf16[8,96,768]{2,1,0:T(8,128)(2,1)S(1)}, u32[]{:S(2)}, u32[]{:S(2)}) collective-permute-start(bf16[8,96,768]{2,1,0:T(8,128)(2,1)S(1)} %copy-done.53), channel_id=1, source_target_pairs={{0,2},{1,5},{2,0},{3,7},{4,6},{5,1},{6,4},{7,3},{8,10},{9,13},{10,... | collective-permute-start | bytes 3538952 | tf_op jit(solution)/shard_map/ppermute | solution.py:316
  58.8 26.8 %collective-permute-start.10 = (bf16[512,1152]{1,0:T(8,128)(2,1)S(1)}, bf16[512,1152]{1,0:T(8,128)(2,1)S(1)}, u32[]{:S(2)}, u32[]{:S(2)}) collective-permute-start(bf16[512,1152]{1,0:T(8,128)(2,1)S(1)} %get-tuple-element.53.grad_qkv), channel_id=1, source_target_pairs={{0,1},{1,0},{2,3},{3,2},{4,5},{5,4},{6,7},{7,6},{8,9},{9,8},{10,11... | collective-permute-start | bytes 3538952 | tf_op jit(solution)/shard_map/ppermute | solution.py:307
  65.2 18.6 %copy-start.33 = (bf16[8,96,768]{2,1,0:T(8,128)(2,1)S(1)}, bf16[8,96,768]{2,1,0:T(8,128)(2,1)}, u32[]{:S(2)}) copy-start(bf16[8,96,768]{2,1,0:T(8,128)(2,1)} %get-tuple-element.65) | copy-start | bytes 3538948
  65.2 29.5 %collective-permute-start.26 = (bf16[4,96,768]{2,1,0:T(8,128)(2,1)S(1)}, bf16[4,96,768]{2,1,0:T(8,128)(2,1)S(1)}, u32[]{:S(2)}, u32[]{:S(2)}) collective-permute-start(bf16[4,96,768]{2,1,0:T(8,128)(2,1)S(1)} %slice.224), channel_id=1, source_target_pairs={{0,4},{1,3},{2,6},{3,1},{4,0},{5,7},{6,2},{7,5},{8,12},{9,11},{10,... | collective-permute-start | bytes 1769480 | tf_op jit(solution)/shard_map/ppermute | solution.py:316
  84.2 12.1 %collective-permute-start.34 = (bf16[4,96,768]{2,1,0:T(8,128)(2,1)S(1)}, bf16[4,96,768]{2,1,0:T(8,128)(2,1)S(1)}, u32[]{:S(2)}, u32[]{:S(2)}) collective-permute-start(bf16[4,96,768]{2,1,0:T(8,128)(2,1)S(1)} %slice.230), channel_id=1, source_target_pairs={{0,4},{1,3},{2,6},{3,1},{4,0},{5,7},{6,2},{7,5},{8,12},{9,11},{10,... | collective-permute-start | bytes 1769480 | tf_op jit(solution)/shard_map/ppermute | solution.py:316
  92.9 15.4 %collective-permute-start.17 = (bf16[8,48,1536]{2,1,0:T(8,128)(2,1)S(1)}, bf16[8,48,1536]{2,1,0:T(8,128)(2,1)S(1)}, u32[]{:S(2)}, u32[]{:S(2)}) collective-permute-start(bf16[8,48,1536]{2,1,0:T(8,128)(2,1)S(1)} %get-tuple-element.60), channel_id=1, source_target_pairs={{0,2},{1,5},{2,0},{3,7},{4,6},{5,1},{6,4},{7,3},{8,10},{9,13},{10,... | collective-permute-start | bytes 3538952 | tf_op jit(solution)/shard_map/ppermute | solution.py:316
  94.8 7.0 %collective-permute-start.27 = (bf16[2,96,768]{2,1,0:T(8,128)(2,1)S(1)}, bf16[2,96,768]{2,1,0:T(8,128)(2,1)S(1)}, u32[]{:S(2)}, u32[]{:S(2)}) collective-permute-start(bf16[2,96,768]{2,1,0:T(8,128)(2,1)S(1)} %slice.226), channel_id=1, source_target_pairs={{0,8},{1,9},{2,10},{3,11},{4,12},{5,13},{6,14},{7,15},{8,0},{9,1},... | collective-permute-start | bytes 884744 | tf_op jit(solution)/shard_map/ppermute | solution.py:316
  96.3 13.4 %collective-permute-start.35 = (bf16[2,96,768]{2,1,0:T(8,128)(2,1)S(1)}, bf16[2,96,768]{2,1,0:T(8,128)(2,1)S(1)}, u32[]{:S(2)}, u32[]{:S(2)}) collective-permute-start(bf16[2,96,768]{2,1,0:T(8,128)(2,1)S(1)} %slice.232), channel_id=1, source_target_pairs={{0,8},{1,9},{2,10},{3,11},{4,12},{5,13},{6,14},{7,15},{8,0},{9,1},... | collective-permute-start | bytes 884744 | tf_op jit(solution)/shard_map/ppermute | solution.py:316
  101.9 9.8 %collective-permute-start.28 = (bf16[1,96,768]{2,1,0:T(8,128)(2,1)S(1)}, bf16[1,96,768]{2,1,0:T(8,128)(2,1)S(1)}, u32[]{:S(2)}, u32[]{:S(2)}) collective-permute-start(bf16[1,96,768]{2,1,0:T(8,128)(2,1)S(1)} %slice.228), channel_id=1, source_target_pairs={{0,16},{1,17},{2,18},{3,19},{4,20},{5,21},{6,22},{7,23},{8,24},{9,... | collective-permute-start | bytes 442376 | tf_op jit(solution)/shard_map/ppermute | solution.py:316
  108.7 14.4 %collective-permute-start.18 = (bf16[4,48,1536]{2,1,0:T(8,128)(2,1)S(1)}, bf16[4,48,1536]{2,1,0:T(8,128)(2,1)S(1)}, u32[]{:S(2)}, u32[]{:S(2)}) collective-permute-start(bf16[4,48,1536]{2,1,0:T(8,128)(2,1)S(1)} %slice.213), channel_id=1, source_target_pairs={{0,4},{1,3},{2,6},{3,1},{4,0},{5,7},{6,2},{7,5},{8,12},{9,11},{10,... | collective-permute-start | bytes 1769480 | tf_op jit(solution)/shard_map/ppermute | solution.py:316
  109.8 13.2 %collective-permute-start.36 = (bf16[1,96,768]{2,1,0:T(8,128)(2,1)S(1)}, bf16[1,96,768]{2,1,0:T(8,128)(2,1)S(1)}, u32[]{:S(2)}, u32[]{:S(2)}) collective-permute-start(bf16[1,96,768]{2,1,0:T(8,128)(2,1)S(1)} %slice.234), channel_id=1, source_target_pairs={{0,16},{1,17},{2,18},{3,19},{4,20},{5,21},{6,22},{7,23},{8,24},{9,... | collective-permute-start | bytes 442376 | tf_op jit(solution)/shard_map/ppermute | solution.py:316
  111.7 22.6 %collective-permute-start.29 = (bf16[1,96,768]{2,1,0:T(8,128)(2,1)S(1)}, bf16[1,96,768]{2,1,0:T(8,128)(2,1)S(1)}, u32[]{:S(2)}, u32[]{:S(2)}) collective-permute-start(bf16[1,96,768]{2,1,0:T(8,128)(2,1)S(1)} %slice_add_fusion.7), channel_id=1, source_target_pairs={{0,16},{1,17},{2,18},{3,19},{4,20},{5,21},{6,22},{7,23},{8,24},{9,... | collective-permute-start | bytes 442376 | tf_op jit(solution)/shard_map/ppermute | solution.py:316
  122.9 11.5 %collective-permute-start.37 = (bf16[1,96,768]{2,1,0:T(8,128)(2,1)S(1)}, bf16[1,96,768]{2,1,0:T(8,128)(2,1)S(1)}, u32[]{:S(2)}, u32[]{:S(2)}) collective-permute-start(bf16[1,96,768]{2,1,0:T(8,128)(2,1)S(1)} %slice_add_fusion.6), channel_id=1, source_target_pairs={{0,16},{1,17},{2,18},{3,19},{4,20},{5,21},{6,22},{7,23},{8,24},{9,... | collective-permute-start | bytes 442376 | tf_op jit(solution)/shard_map/ppermute | solution.py:316
  123.1 13.5 %collective-permute-start.19 = (bf16[2,48,1536]{2,1,0:T(8,128)(2,1)S(1)}, bf16[2,48,1536]{2,1,0:T(8,128)(2,1)}, u32[]{:S(2)}, u32[]{:S(2)}) collective-permute-start(bf16[2,48,1536]{2,1,0:T(8,128)(2,1)S(1)} %slice.215), channel_id=1, source_target_pairs={{0,8},{1,9},{2,10},{3,11},{4,12},{5,13},{6,14},{7,15},{8,0},{9,1},... | collective-permute-start | bytes 884744 | tf_op jit(solution)/shard_map/ppermute | solution.py:316
  126.4 9.6 %copy-start.18 = (f32[256,768]{1,0:T(8,128)S(1)}, f32[256,768]{1,0:T(8,128)}, u32[]{:S(2)}) copy-start(f32[256,768]{1,0:T(8,128)} %copy-done.17) | copy-start | bytes 2359300
  126.5 54.7 %collective-permute-start.7 = (f32[256,768]{1,0:T(8,128)}, f32[256,768]{1,0:T(8,128)S(1)}, u32[]{:S(2)}, u32[]{:S(2)}) collective-permute-start(f32[256,768]{1,0:T(8,128)} %convolution_add_fusion.2), channel_id=1, source_target_pairs={{0,1},{1,0},{2,3},{3,2},{4,5},{5,4},{6,7},{7,6},{8,9},{9,8},{10,11... | collective-permute-start | bytes 2359304 | tf_op jit(solution)/shard_map/ppermute | solution.py:307
  134.4 12.2 %collective-permute-start.30 = (bf16[2,96,768]{2,1,0:T(8,128)(2,1)S(1)}, bf16[2,96,768]{2,1,0:T(8,128)(2,1)S(1)}, u32[]{:S(2)}, u32[]{:S(2)}) collective-permute-start(bf16[2,96,768]{2,1,0:T(8,128)(2,1)S(1)} %pad_maximum_fusion.8), channel_id=1, source_target_pairs={{0,8},{1,9},{2,10},{3,11},{4,12},{5,13},{6,14},{7,15},{8,0},{9,1},... | collective-permute-start | bytes 884744 | tf_op jit(solution)/shard_map/ppermute | solution.py:316
  134.5 18.4 %collective-permute-start.38 = (bf16[2,96,768]{2,1,0:T(8,128)(2,1)S(1)}, bf16[2,96,768]{2,1,0:T(8,128)(2,1)S(1)}, u32[]{:S(2)}, u32[]{:S(2)}) collective-permute-start(bf16[2,96,768]{2,1,0:T(8,128)(2,1)S(1)} %pad_maximum_fusion.9), channel_id=1, source_target_pairs={{0,8},{1,9},{2,10},{3,11},{4,12},{5,13},{6,14},{7,15},{8,0},{9,1},... | collective-permute-start | bytes 884744 | tf_op jit(solution)/shard_map/ppermute | solution.py:316
  136.0 17.6 %collective-permute-start.11 = (f32[256,768]{1,0:T(8,128)S(1)}, f32[256,768]{1,0:T(8,128)S(1)}, u32[]{:S(2)}, u32[]{:S(2)}) collective-permute-start(f32[256,768]{1,0:T(8,128)S(1)} %copy-done.18), channel_id=1, source_target_pairs={{0,1},{1,0},{2,3},{3,2},{4,5},{5,4},{6,7},{7,6},{8,9},{9,8},{10,11... | collective-permute-start | bytes 2359304 | tf_op jit(solution)/shard_map/ppermute | solution.py:307
  137.6 16.0 %copy-start.6 = (f32[256,768]{1,0:T(8,128)S(1)}, f32[256,768]{1,0:T(8,128)}, u32[]{:S(2)}) copy-start(f32[256,768]{1,0:T(8,128)} %copy-done.5) | copy-start | bytes 2359300
  137.6 16.0 %copy-start.43 = (f32[256]{0:T(256)S(1)}, f32[256]{0:T(256)}, u32[]{:S(2)}) copy-start(f32[256]{0:T(256)} %add_rsqrt_fusion) | copy-start | bytes 3076
  137.7 15.4 %collective-permute-start.20 = (bf16[1,48,1536]{2,1,0:T(8,128)(2,1)S(1)}, bf16[1,48,1536]{2,1,0:T(8,128)(2,1)S(1)}, u32[]{:S(2)}, u32[]{:S(2)}) collective-permute-start(bf16[1,48,1536]{2,1,0:T(8,128)(2,1)S(1)} %slice.217), channel_id=1, source_target_pairs={{0,16},{1,17},{2,18},{3,19},{4,20},{5,21},{6,22},{7,23},{8,24},{9,... | collective-permute-start | bytes 442376 | tf_op jit(solution)/shard_map/ppermute | solution.py:316
  146.7 24.0 %collective-permute-start.31 = (bf16[4,96,768]{2,1,0:T(8,128)(2,1)S(1)}, bf16[4,96,768]{2,1,0:T(8,128)(2,1)S(1)}, u32[]{:S(2)}, u32[]{:S(2)}) collective-permute-start(bf16[4,96,768]{2,1,0:T(8,128)(2,1)S(1)} %pad_maximum_fusion.4), channel_id=1, source_target_pairs={{0,4},{1,3},{2,6},{3,1},{4,0},{5,7},{6,2},{7,5},{8,12},{9,11},{10,... | collective-permute-start | bytes 1769480 | tf_op jit(solution)/shard_map/ppermute | solution.py:316
  153.0 18.9 %collective-permute-start.39 = (bf16[4,96,768]{2,1,0:T(8,128)(2,1)S(1)}, bf16[4,96,768]{2,1,0:T(8,128)(2,1)S(1)}, u32[]{:S(2)}, u32[]{:S(2)}) collective-permute-start(bf16[4,96,768]{2,1,0:T(8,128)(2,1)S(1)} %pad_maximum_fusion.5), channel_id=1, source_target_pairs={{0,4},{1,3},{2,6},{3,1},{4,0},{5,7},{6,2},{7,5},{8,12},{9,11},{10,... | collective-permute-start | bytes 1769480 | tf_op jit(solution)/shard_map/ppermute | solution.py:316
  153.1 6.2 %collective-permute-start.21 = (bf16[1,48,1536]{2,1,0:T(8,128)(2,1)S(1)}, bf16[1,48,1536]{2,1,0:T(8,128)(2,1)S(1)}, u32[]{:S(2)}, u32[]{:S(2)}) collective-permute-start(bf16[1,48,1536]{2,1,0:T(8,128)(2,1)S(1)} %slice_add_fusion.8), channel_id=1, source_target_pairs={{0,16},{1,17},{2,18},{3,19},{4,20},{5,21},{6,22},{7,23},{8,24},{9,... | collective-permute-start | bytes 442376 | tf_op jit(solution)/shard_map/ppermute | solution.py:316
  159.4 5.9 %collective-permute-start.22 = (bf16[2,48,1536]{2,1,0:T(8,128)(2,1)S(1)}, bf16[2,48,1536]{2,1,0:T(8,128)(2,1)S(1)}, u32[]{:S(2)}, u32[]{:S(2)}) collective-permute-start(bf16[2,48,1536]{2,1,0:T(8,128)(2,1)S(1)} %pad_maximum_fusion.7), channel_id=1, source_target_pairs={{0,8},{1,9},{2,10},{3,11},{4,12},{5,13},{6,14},{7,15},{8,0},{9,1},... | collective-permute-start | bytes 884744 | tf_op jit(solution)/shard_map/ppermute | solution.py:316
  159.6 11.0 %collective-permute-start.12 = (f32[6,384]{1,0:T(8,128)S(1)}, f32[6,384]{1,0:T(8,128)S(1)}, u32[]{:S(2)}, u32[]{:S(2)}) collective-permute-start(f32[6,384]{1,0:T(8,128)S(1)} %slice_select_fusion), channel_id=1, source_target_pairs={{0,1},{1,0},{2,3},{3,2},{4,5},{5,4},{6,7},{7,6},{8,9},{9,8},{10,11... | collective-permute-start | bytes 27656 | tf_op jit(solution)/shard_map/ppermute | solution.py:307
  165.3 14.5 %collective-permute-start.23 = (bf16[4,48,1536]{2,1,0:T(8,128)(2,1)S(1)}, bf16[4,48,1536]{2,1,0:T(8,128)(2,1)S(1)}, u32[]{:S(2)}, u32[]{:S(2)}) collective-permute-start(bf16[4,48,1536]{2,1,0:T(8,128)(2,1)S(1)} %pad_maximum_fusion.3), channel_id=1, source_target_pairs={{0,4},{1,3},{2,6},{3,1},{4,0},{5,7},{6,2},{7,5},{8,12},{9,11},{10,... | collective-permute-start | bytes 1769480 | tf_op jit(solution)/shard_map/ppermute | solution.py:316
  170.6 11.8 %collective-permute-start.13 = (f32[12,384]{1,0:T(8,128)S(1)}, f32[12,384]{1,0:T(8,128)S(1)}, u32[]{:S(2)}, u32[]{:S(2)}) collective-permute-start(f32[12,384]{1,0:T(8,128)S(1)} %pad_maximum_fusion.10), channel_id=1, source_target_pairs={{0,2},{2,0},{4,6},{6,4},{8,10},{10,8},{12,14},{14,12},{16,18},{18,... | collective-permute-start | bytes 55304 | tf_op jit(solution)/shard_map/ppermute | solution.py:307
  170.9 62.0 %collective-permute-start.32 = (bf16[8,96,768]{2,1,0:T(8,128)(2,1)S(1)}, bf16[8,96,768]{2,1,0:T(8,128)(2,1)}, u32[]{:S(2)}, u32[]{:S(2)}) collective-permute-start(bf16[8,96,768]{2,1,0:T(8,128)(2,1)S(1)} %pad_maximum_fusion.1.own_ref), channel_id=1, source_target_pairs={{0,2},{1,5},{2,0},{3,7},{4,6},{5,1},{6,4},{7,3},{8,10},{9,13},{10,... | collective-permute-start | bytes 3538952 | tf_op jit(solution)/shard_map/ppermute | solution.py:316
  173.0 52.7 %collective-permute-start.40 = (bf16[8,96,768]{2,1,0:T(8,128)(2,1)}, bf16[8,96,768]{2,1,0:T(8,128)(2,1)}, u32[]{:S(2)}, u32[]{:S(2)}) collective-permute-start(bf16[8,96,768]{2,1,0:T(8,128)(2,1)} %pad_maximum_fusion.2.own_ref), channel_id=1, source_target_pairs={{0,2},{1,5},{2,0},{3,7},{4,6},{5,1},{6,4},{7,3},{8,10},{9,13},{10,... | collective-permute-start | bytes 3538952 | tf_op jit(solution)/shard_map/ppermute | solution.py:316
  180.0 60.0 %collective-permute-start.24 = (bf16[8,48,1536]{2,1,0:T(8,128)(2,1)S(1)}, bf16[8,48,1536]{2,1,0:T(8,128)(2,1)}, u32[]{:S(2)}, u32[]{:S(2)}) collective-permute-start(bf16[8,48,1536]{2,1,0:T(8,128)(2,1)S(1)} %pad_maximum_fusion.own_ref), channel_id=1, source_target_pairs={{0,2},{1,5},{2,0},{3,7},{4,6},{5,1},{6,4},{7,3},{8,10},{9,13},{10,... | collective-permute-start | bytes 3538952 | tf_op jit(solution)/shard_map/ppermute | solution.py:316
  181.2 40.7 %copy-start.30 = (f32[256,768]{1,0:T(8,128)S(1)}, f32[256,768]{1,0:T(8,128)}, u32[]{:S(2)}) copy-start(f32[256,768]{1,0:T(8,128)} %copy-done.29) | copy-start | bytes 2359300
  182.5 35.6 %collective-permute-start.14 = (f32[12,384]{1,0:T(8,128)S(1)}, f32[12,384]{1,0:T(8,128)S(1)}, u32[]{:S(2)}, u32[]{:S(2)}) collective-permute-start(f32[12,384]{1,0:T(8,128)S(1)} %fusion.32), channel_id=1, source_target_pairs={{0,4},{2,6},{4,0},{6,2},{8,12},{10,14},{12,8},{14,10},{16,20},{18,... | collective-permute-start | bytes 55304 | tf_op jit(solution)/shard_map/ppermute | solution.py:307
  218.1 2.7 %collective-permute-start.15 = (f32[12,384]{1,0:T(8,128)S(1)}, f32[12,384]{1,0:T(8,128)S(1)}, u32[]{:S(2)}, u32[]{:S(2)}) collective-permute-start(f32[12,384]{1,0:T(8,128)S(1)} %add.210), channel_id=1, source_target_pairs={{0,8},{2,10},{4,12},{6,14},{8,0},{10,2},{12,4},{14,6},{16,24},{18,... | collective-permute-start | bytes 55304 | tf_op jit(solution)/shard_map/ppermute | solution.py:307
  220.8 3.7 %collective-permute-start.16 = (f32[12,384]{1,0:T(8,128)S(1)}, f32[12,384]{1,0:T(8,128)S(1)}, u32[]{:S(2)}, u32[]{:S(2)}) collective-permute-start(f32[12,384]{1,0:T(8,128)S(1)} %add.211), channel_id=1, source_target_pairs={{0,16},{2,18},{4,20},{6,22},{8,24},{10,26},{12,28},{14,30},{16,0},... | collective-permute-start | bytes 55304 | tf_op jit(solution)/shard_map/ppermute | solution.py:307
  (47 other events, 198.2 us)
